TPU v7x, 32 devices: a whole 2x2x4 slice. The times are simulated.
32 devices in a mesh: dp: 8 (over y, x, core), seq: 4 (over z).
Axes of the slice: x: 2, y: 2, z: 4, core: 2. Of those that a mesh axis runs over, the one named last changes fastest.
Arguments:
- tokens_in: bfloat16 [16, 580, 1024], P('dp', 'seq'), may hold values from -6 to 6
- cotangent: bfloat16 [16, 580, 1024], P('dp', 'seq'), may hold values from -6 to 6
- group_count: int32 [8], P('dp'), may hold values from 1 to 2, as said below
- key_mask: int32 [16, 580], P('dp'), may hold values from 0 to 1, as said below
- ln1_gain: float32 [1024], P(('dp', 'seq')), may hold values from 0.5 to 1.5
- ln1_shift: float32 [1024], P(('dp', 'seq')), may hold values from -3 to 3
- w_query: float32 [1024, 1024], P(('dp', 'seq')), may hold values from -0.25 to 0.25
- b_query: float32 [1024], P(('dp', 'seq')), may hold values from -3 to 3
- w_key: float32 [1024, 1024], P(('dp', 'seq')), may hold values from -0.1875 to 0.1875
- w_value: float32 [1024, 1024], P(('dp', 'seq')), may hold values from -0.1875 to 0.1875
- b_value: float32 [1024], P(('dp', 'seq')), may hold values from -0.6 to 0.6
- w_out: float32 [1024, 1024], P(('dp', 'seq')), may hold values from -1.5 to 1.5
- b_out: float32 [1024], P(('dp', 'seq')), may hold values from -3 to 3
- ln2_gain: float32 [1024], P(('dp', 'seq')), may hold values from 0.5 to 1.5
- ln2_shift: float32 [1024], P(('dp', 'seq')), may hold values from -3 to 3
- w_up: float32 [1024, 4096], P(('dp', 'seq')), may hold values from -0.1875 to 0.1875
- b_up: float32 [4096], P(('dp', 'seq')), may hold values from -3 to 3
- w_down: float32 [4096, 1024], P(('dp', 'seq')), may hold values from -0.09375 to 0.09375
- b_down: float32 [1024], P(('dp', 'seq')), may hold values from -3 to 3
Outputs:
- block_out: bfloat16 [16, 580, 1024], P('dp', 'seq')
- input_grad: bfloat16 [16, 580, 1024], P('dp', 'seq')
- grad_ln1_gain: float32 [1024], P(('dp', 'seq'))
- grad_ln1_shift: float32 [1024], P(('dp', 'seq'))
- grad_w_query: float32 [1024, 1024], P(('dp', 'seq'))
- grad_b_query: float32 [1024], P(('dp', 'seq'))
- grad_w_key: float32 [1024, 1024], P(('dp', 'seq'))
- grad_w_value: float32 [1024, 1024], P(('dp', 'seq'))
- grad_b_value: float32 [1024], P(('dp', 'seq'))
- grad_w_out: float32 [1024, 1024], P(('dp', 'seq'))
- grad_b_out: float32 [1024], P(('dp', 'seq'))
- grad_ln2_gain: float32 [1024], P(('dp', 'seq'))
- grad_ln2_shift: float32 [1024], P(('dp', 'seq'))
- grad_w_up: float32 [1024, 4096], P(('dp', 'seq'))
- grad_b_up: float32 [4096], P(('dp', 'seq'))
- grad_w_down: float32 [4096, 1024], P(('dp', 'seq'))
- grad_b_down: float32 [1024], P(('dp', 'seq'))
Inputs may be any that keep to these rules, and one draw needn't show every extreme that they name: A data group's images fill its first group_count slots; some group holds 2. `key_mask`: the first token of every image is a key; positions 577 and later never are.
All inputs are finite; a program needn't handle non-finite values.
Results may differ from a plain program's by a relative error of at most 0.013.
The roundings to bfloat16 on the way count: a program that leaves them out, or rounds other values in their place, can miss the bound.
Values may be sent and summed in bfloat16 or wider, within the bound.
No kernel may reach another device: no remote copies, remote signals or barrier semaphores. Data moves between devices by JAX's collectives and lax.ppermute only.
A program may use at most 192 MiB of HBM per device.

v0:
```python
import jax
import jax.numpy as jnp
from jax import lax
from jax.sharding import PartitionSpec as P

HD = 64


EPSILON = 1e-05
SLOPE = 1.702
MASKED = -1000000000.0


def norm_stats(values):
    center = values - jnp.mean(values, axis=-1, keepdims=True)
    inverse = lax.rsqrt(jnp.mean(center * center, axis=-1, keepdims=True) + EPSILON)
    return (center * inverse, inverse)


def norm_back(incoming, normal, inverse, gain):
    scaled = incoming * gain
    rows_grad = inverse * (
        scaled
        - jnp.mean(scaled, axis=-1, keepdims=True)
        - normal * jnp.mean(scaled * normal, axis=-1, keepdims=True)
    )
    return (rows_grad, jnp.sum(incoming * normal, axis=0), jnp.sum(incoming, axis=0))


def product(left, right):
    return jnp.dot(left, right, preferred_element_type=jnp.float32)


def contract_rows(left, right):
    return lax.dot_general(
        left, right, (((0,), (0,)), ((), ())), preferred_element_type=jnp.float32
    )


def contract_cols(left, right):
    return lax.dot_general(
        left, right, (((1,), (1,)), ((), ())), preferred_element_type=jnp.float32
    )


def split_heads(stacked):
    length = stacked.shape[0]
    heads_here = stacked.shape[2] // HD
    queries = stacked[:, 0].reshape(length, heads_here, HD)
    keys_all = stacked[:, 1].reshape(length, heads_here, HD)
    values_all = stacked[:, 2].reshape(length, heads_here, HD)
    return (queries, keys_all, values_all)


def masked_scores(queries, keys_all, key_keep):
    scores = jnp.einsum(
        "qhd,khd->hqk", queries, keys_all, preferred_element_type=jnp.float32
    ) * HD ** (-0.5)
    return jnp.where(key_keep[None, None, :] > 0, scores, MASKED)


def attend_image(paired):
    stacked, key_keep = paired
    queries, keys_all, values_all = split_heads(stacked)
    scores = masked_scores(queries, keys_all, key_keep)
    row_peak = jnp.max(scores, axis=-1, keepdims=True)
    weights_exp = jnp.exp(scores - row_peak)
    row_total = jnp.sum(weights_exp, axis=-1, keepdims=True)
    weights_soft = weights_exp / row_total
    mixed_out = jnp.einsum(
        "hqk,khd->qhd",
        weights_soft.astype(jnp.bfloat16),
        values_all,
        preferred_element_type=jnp.float32,
    )
    log_total = (row_peak + jnp.log(row_total))[..., 0]
    return (mixed_out.reshape(stacked.shape[0], stacked.shape[2]).astype(jnp.bfloat16), log_total)


def attend_back(packed):
    stacked, grad_mixed, log_total, key_keep = packed
    queries, keys_all, values_all = split_heads(stacked)
    scores = masked_scores(queries, keys_all, key_keep)
    weights_soft = jnp.exp(scores - log_total[..., None])
    grad_mix = grad_mixed.reshape(queries.shape)
    grad_values = jnp.einsum(
        "hqk,qhd->khd",
        weights_soft.astype(jnp.bfloat16),
        grad_mix,
        preferred_element_type=jnp.float32,
    )
    grad_weights = jnp.einsum(
        "qhd,khd->hqk", grad_mix, values_all, preferred_element_type=jnp.float32
    )
    row_inner = jnp.sum(grad_weights * weights_soft, axis=-1, keepdims=True)
    grad_scores = (weights_soft * (grad_weights - row_inner)).astype(jnp.bfloat16)
    grad_queries = jnp.einsum(
        "hqk,khd->qhd", grad_scores, keys_all, preferred_element_type=jnp.float32
    ) * HD ** (-0.5)
    grad_keys = jnp.einsum(
        "hqk,qhd->khd", grad_scores, queries, preferred_element_type=jnp.float32
    ) * HD ** (-0.5)
    length = stacked.shape[0]
    return jnp.stack(
        [
            grad_queries.reshape(length, -1),
            grad_keys.reshape(length, -1),
            grad_values.reshape(length, -1),
        ],
        axis=1,
    ).astype(jnp.bfloat16)


def per_device(
    tokens_in,
    cotangent,
    group_count,
    key_mask,
    ln1_gain,
    ln1_shift,
    w_query,
    b_query,
    w_key,
    w_value,
    b_value,
    w_out,
    b_out,
    ln2_gain,
    ln2_shift,
    w_up,
    b_up,
    w_down,
    b_down,
):
    slot_count, tok_dev, width = tokens_in.shape
    row_count = slot_count * tok_dev
    shared = (
        lax.all_gather(ln1_gain.astype(jnp.bfloat16), ("dp", "seq"), axis=0, tiled=True),
        lax.all_gather(ln1_shift.astype(jnp.bfloat16), ("dp", "seq"), axis=0, tiled=True),
        lax.all_gather(w_query.astype(jnp.bfloat16), ("dp", "seq"), axis=0, tiled=True),
        lax.all_gather(b_query.astype(jnp.bfloat16), ("dp", "seq"), axis=0, tiled=True),
        lax.all_gather(w_key.astype(jnp.bfloat16), ("dp", "seq"), axis=0, tiled=True),
        lax.all_gather(w_value.astype(jnp.bfloat16), ("dp", "seq"), axis=0, tiled=True),
        lax.all_gather(b_value.astype(jnp.bfloat16), ("dp", "seq"), axis=0, tiled=True),
        lax.all_gather(w_out.astype(jnp.bfloat16), ("dp", "seq"), axis=0, tiled=True),
        lax.all_gather(b_out.astype(jnp.bfloat16), ("dp", "seq"), axis=0, tiled=True),
        lax.all_gather(ln2_gain.astype(jnp.bfloat16), ("dp", "seq"), axis=0, tiled=True),
        lax.all_gather(ln2_shift.astype(jnp.bfloat16), ("dp", "seq"), axis=0, tiled=True),
        lax.all_gather(w_up.astype(jnp.bfloat16), ("dp", "seq"), axis=0, tiled=True),
        lax.all_gather(b_up.astype(jnp.bfloat16), ("dp", "seq"), axis=0, tiled=True),
        lax.all_gather(w_down.astype(jnp.bfloat16), ("dp", "seq"), axis=0, tiled=True),
        lax.all_gather(b_down.astype(jnp.bfloat16), ("dp", "seq"), axis=0, tiled=True),
    )
    (
        gain_one,
        shift_one,
        query_w,
        query_b,
        key_w,
        value_w,
        value_b,
        out_w,
        out_b,
        gain_two,
        shift_two,
        up_w,
        up_b,
        down_w,
        down_b,
    ) = shared
    live_slot = (jnp.arange(slot_count) < group_count[0]).astype(jnp.float32)[:, None, None]
    inputs = tokens_in.astype(jnp.float32).reshape(row_count, width)
    normal_one, inverse_one = norm_stats(inputs)
    normed_one = (normal_one * gain_one + shift_one).astype(jnp.bfloat16)
    queries = (product(normed_one, query_w) + query_b).astype(jnp.bfloat16)
    keys_all = product(normed_one, key_w).astype(jnp.bfloat16)
    values_all = (product(normed_one, value_w) + value_b).astype(jnp.bfloat16)
    stacked = jnp.stack([queries, keys_all, values_all], axis=1).reshape(
        slot_count, tok_dev, 3, width
    )
    by_heads = lax.all_to_all(stacked, "seq", split_axis=3, concat_axis=1, tiled=True)
    mixed_heads, log_total = lax.map(attend_image, (by_heads, key_mask))
    mixed_tok = lax.all_to_all(mixed_heads, "seq", split_axis=1, concat_axis=2, tiled=True).reshape(
        row_count, width
    )
    middle = inputs + product(mixed_tok, out_w) + out_b
    normal_two, inverse_two = norm_stats(middle)
    normed_two = (normal_two * gain_two + shift_two).astype(jnp.bfloat16)
    hidden = product(normed_two, up_w) + up_b
    gate_sig = jax.nn.sigmoid(SLOPE * hidden)
    activated = (hidden * gate_sig).astype(jnp.bfloat16)
    result = middle + product(activated, down_w) + down_b
    block_out = (result.reshape(slot_count, tok_dev, width) * live_slot).astype(jnp.bfloat16)
    upstream = (cotangent.astype(jnp.float32) * live_slot).reshape(row_count, width)
    upstream_low = upstream.astype(jnp.bfloat16)
    grad_down = contract_rows(activated, upstream_low)
    grad_down_b = jnp.sum(upstream, axis=0)
    grad_act = contract_cols(upstream_low, down_w)
    grad_hidden = (grad_act * (gate_sig + SLOPE * hidden * gate_sig * (1.0 - gate_sig))).astype(
        jnp.bfloat16
    )
    grad_up = contract_rows(normed_two, grad_hidden)
    grad_up_b = jnp.sum(grad_hidden.astype(jnp.float32), axis=0)
    grad_normed_two = contract_cols(grad_hidden, up_w)
    grad_mid, grad_gain_two, grad_shift_two = norm_back(
        grad_normed_two, normal_two, inverse_two, gain_two
    )
    grad_middle = upstream + grad_mid
    branch_low = grad_middle.astype(jnp.bfloat16)
    grad_out = contract_rows(mixed_tok, branch_low)
    grad_out_b = jnp.sum(branch_low.astype(jnp.float32), axis=0)
    grad_mixed = (
        contract_cols(branch_low, out_w).astype(jnp.bfloat16).reshape(slot_count, tok_dev, width)
    )
    grad_by_heads = lax.all_to_all(grad_mixed, "seq", split_axis=2, concat_axis=1, tiled=True)
    grad_stacked = lax.map(attend_back, (by_heads, grad_by_heads, log_total, key_mask))
    grad_tok = lax.all_to_all(grad_stacked, "seq", split_axis=1, concat_axis=3, tiled=True).reshape(
        row_count, 3, width
    )
    grad_q_rows = grad_tok[:, 0]
    grad_k_rows = grad_tok[:, 1]
    grad_v_rows = grad_tok[:, 2]
    grad_query = contract_rows(normed_one, grad_q_rows)
    grad_query_b = jnp.sum(grad_q_rows.astype(jnp.float32), axis=0)
    grad_key = contract_rows(normed_one, grad_k_rows)
    grad_value = contract_rows(normed_one, grad_v_rows)
    grad_value_b = jnp.sum(grad_v_rows.astype(jnp.float32), axis=0)
    grad_normed_one = (
        contract_cols(grad_q_rows, query_w)
        + contract_cols(grad_k_rows, key_w)
        + contract_cols(grad_v_rows, value_w)
    )
    grad_first, grad_gain_one, grad_shift_one = norm_back(
        grad_normed_one, normal_one, inverse_one, gain_one
    )
    input_grad = (grad_middle + grad_first).astype(jnp.bfloat16).reshape(slot_count, tok_dev, width)
    every_shard = (
        lax.psum_scatter(grad_gain_one, ("dp", "seq"), scatter_dimension=0, tiled=True),
        lax.psum_scatter(grad_shift_one, ("dp", "seq"), scatter_dimension=0, tiled=True),
        lax.psum_scatter(grad_query, ("dp", "seq"), scatter_dimension=0, tiled=True),
        lax.psum_scatter(grad_query_b, ("dp", "seq"), scatter_dimension=0, tiled=True),
        lax.psum_scatter(grad_key, ("dp", "seq"), scatter_dimension=0, tiled=True),
        lax.psum_scatter(grad_value, ("dp", "seq"), scatter_dimension=0, tiled=True),
        lax.psum_scatter(grad_value_b, ("dp", "seq"), scatter_dimension=0, tiled=True),
        lax.psum_scatter(grad_out, ("dp", "seq"), scatter_dimension=0, tiled=True),
        lax.psum_scatter(grad_out_b, ("dp", "seq"), scatter_dimension=0, tiled=True),
        lax.psum_scatter(grad_gain_two, ("dp", "seq"), scatter_dimension=0, tiled=True),
        lax.psum_scatter(grad_shift_two, ("dp", "seq"), scatter_dimension=0, tiled=True),
        lax.psum_scatter(grad_up, ("dp", "seq"), scatter_dimension=0, tiled=True),
        lax.psum_scatter(grad_up_b, ("dp", "seq"), scatter_dimension=0, tiled=True),
        lax.psum_scatter(grad_down, ("dp", "seq"), scatter_dimension=0, tiled=True),
        lax.psum_scatter(grad_down_b, ("dp", "seq"), scatter_dimension=0, tiled=True),
    )
    return (block_out, input_grad) + tuple(every_shard)


def solution(mesh):
    return jax.shard_map(
        per_device,
        mesh=mesh,
        in_specs=(
            P("dp", "seq", None),
            P("dp", "seq", None),
            P("dp"),
            P("dp", None),
            P(("dp", "seq")),
            P(("dp", "seq")),
            P(("dp", "seq"), None),
            P(("dp", "seq")),
            P(("dp", "seq"), None),
            P(("dp", "seq"), None),
            P(("dp", "seq")),
            P(("dp", "seq"), None),
            P(("dp", "seq")),
            P(("dp", "seq")),
            P(("dp", "seq")),
            P(("dp", "seq"), None),
            P(("dp", "seq")),
            P(("dp", "seq"), None),
            P(("dp", "seq")),
        ),
        out_specs=(
            P("dp", "seq", None),
            P("dp", "seq", None),
            P(("dp", "seq")),
            P(("dp", "seq")),
            P(("dp", "seq"), None),
            P(("dp", "seq")),
            P(("dp", "seq"), None),
            P(("dp", "seq"), None),
            P(("dp", "seq")),
            P(("dp", "seq"), None),
            P(("dp", "seq")),
            P(("dp", "seq")),
            P(("dp", "seq")),
            P(("dp", "seq"), None),
            P(("dp", "seq")),
            P(("dp", "seq"), None),
            P(("dp", "seq")),
        ),
        check_vma=False,
    )
```

profile of v0, /device:TPU:0, one launch (start us, length us, event | category | flops | bytes accessed | tf_op | source)
XLA Modules:
  0.0 1860.6 jit_solution(8726085616884812577)
XLA Ops:
  7.3 1.7 convert_element_type.187
  9.1 1.5 convert_element_type.185
  10.8 1.5 convert_element_type.181
  12.4 1.5 convert_element_type.191
  14.0 1.8 convert_element_type.199
  18.8 42.5 %all-reduce.18 = (bf16[1024]{0:T(1024)(128)(2,1)S(1)}, bf16[1024]{0:T(1024)(128)(2,1)S(1)}, bf16[1024]{0:T(1024)(128)(2,1)S(1)}, bf16[1024]{0:T(1024)(128)(2,1)S...) all-reduce(bf16[1024]{0:T(1024)(128)(2,1)S(1)} %dynamic-update-slic, ...), channel_id=1, replica_groups=mesh['dp'=8,'seq'=4] {'dp','seq'}, use_global_device_ids=true, to_apply=%add.1 | all-reduce | flops 8192 | bytes 32768
  63.5 7.6 all-gather.12.cloned.1.call-done
  71.1 3.2 fusion.21
  75.5 54.4 %all-gather.10.cloned.1.call-done = bf16[1024,1024]{1,0:T(8,128)(2,1)} async-done(((bf16[32,1024]{1,0:T(8,128)(2,1)}), bf16[1024,1024]{1,0:T(8,128)(2,1)}) %all-gather.10.cloned.1.call-update) | async-done | bytes 2097168 | tf_op jit(solution)/shard_map/all_gather | solution.py:142
  129.9 2.4 convolution_convert_fusion.1
  132.5 56.2 %all-gather.8.cloned.1.call-done = bf16[1024,1024]{1,0:T(8,128)(2,1)} async-done(((bf16[32,1024]{1,0:T(8,128)(2,1)}), bf16[1024,1024]{1,0:T(8,128)(2,1)}) %all-gather.8.cloned.1.call-update) | async-done | bytes 2097168 | tf_op jit(solution)/shard_map/all_gather | solution.py:140
  188.7 2.6 fusion.20
  193.5 5.7 copy.101
  199.3 4.2 all-to-all-start
  203.5 80.4 %all-to-all-done = bf16[2,145,3,1024]{1,0,2,3:T(2,128)(2,1)S(1)} async-done(((bf16[2,145,3,1024]{1,0,2,3:T(2,128)(2,1)}), bf16[2,145,3,1024]{1,0,2,3:T(2,128)(2,1)S(1)}, u32[]{:S(2)}, u32[]{:S(2)}) %all-to-all-start) | async-done | bytes 1781792 | tf_op jit(solution)/shard_map/all_to_all | solution.py:181
  283.9 4.1 copy.145
  288.0 5.4 reshape.335
  293.4 9.7 while.22
  293.6 1.4 fusion.98
  296.4 1.7 fusion.100
  301.3 1.7 fusion.100
  304.4 3.5 all-to-all-start.1
  308.6 83.2 %all-gather = bf16[32,1,128]{2,1,0:T(2,128)(2,1)S(1)} all-gather(bf16[1,1,128]{2,1,0:T(2,128)(2,1)S(1)} %convert_bitcast_fusion), channel_id=1, replica_groups=mesh['dp'=8,'seq'=4] {'dp','seq'}, dimensions={0}, use_global_device_ids=true | all-gather | bytes 8448 | tf_op jit(solution)/shard_map/all_gather | solution.py:150
  393.4 3.0 fusion.36
  396.8 8.8 convolution_add_fusion
  405.5 42.2 %all-gather.18.cloned.1.call-done = bf16[4096,1024]{1,0:T(8,128)(2,1)} async-done(((bf16[128,1024]{1,0:T(8,128)(2,1)}), bf16[4096,1024]{1,0:T(8,128)(2,1)}) %all-gather.18.cloned.1.call-update) | async-done | bytes 8388624 | tf_op jit(solution)/shard_map/all_gather | solution.py:151
  447.8 8.7 fusion.19
  456.4 2.5 reshape.310
  458.9 3.7 fusion.32
  462.6 2.4 reshape.311
  465.0 9.0 convert_reduce_fusion
  474.1 6.4 multiply_reduce_fusion.1
  484.4 3.7 copy.109
  488.0 4.3 all-to-all-start.2
  492.4 4.4 fusion.29
  496.8 35.8 %all-to-all-done.2 = bf16[2,145,1024]{1,0,2:T(2,128)(2,1)} async-done(((bf16[2,145,1024]{1,0,2:T(2,128)(2,1)}), bf16[2,145,1024]{1,0,2:T(2,128)(2,1)}, u32[]{:S(2)}, u32[]{:S(2)}) %all-to-all-start.2) | async-done | bytes 593952 | tf_op jit(solution)/shard_map/all_to_all | solution.py:215
  532.5 3.0 copy.147
  535.6 2.5 reshape.334
  538.0 21.9 %while.23 = (s32[]{:T(128)}, bf16[2,580,3,256]{1,3,2,0:T(8,128)(2,1)}, bf16[2,580,3,256]{1,3,2,0:T(8,128)(2,1)S(1)}, s32[2,580]{1,0:T(2,128)S(1)}, f32[2,4,580]{...) while((s32[]{:T(128)}, bf16[2,580,3,256]{1,3,2,0:T(8,128)(2,1)}, ...), condition=%wide.region_12.13_spmd, body=%wide.region_10.12_spmd.sunk | while | flops 884781312 | bytes 63784960 | solution.py:216
  539.5 1.5 fusion.113
  541.0 2.0 multiply_reduce_fusion.10
  543.0 1.9 multiply_convert_fusion.6
  550.4 1.5 fusion.113
  551.9 2.0 multiply_reduce_fusion.10
  554.0 1.9 multiply_convert_fusion.6
  559.9 5.2 copy.114
  565.1 4.5 all-to-all-start.3
  571.1 61.1 %all-to-all-done.3 = bf16[2,580,3,256]{3,0,2,1:T(2,128)(2,1)} async-done(((bf16[2,580,3,256]{3,0,2,1:T(2,128)(2,1)}), bf16[2,580,3,256]{3,0,2,1:T(2,128)(2,1)}, u32[]{:S(2)}, u32[]{:S(2)}) %all-to-all-start.3) | async-done | bytes 1781792 | tf_op jit(solution)/shard_map/all_to_all | solution.py:217
  632.2 1.8 copy.146
  634.0 2.0 copy.116
  635.9 3.2 reshape.313
  639.2 3.3 fusion.23
  642.6 3.3 fusion.22
  645.9 3.4 fusion.25
  650.6 10.1 fusion.33
  661.9 11.0 fusion.26
  675.4 2.6 fusion.24
  681.9 1.4 copy.120
  683.6 40.4 %all-reduce.17 = (f32[1024]{0:T(1024)S(1)}, f32[1024]{0:T(1024)S(1)}, f32[1024]{0:T(1024)S(1)}, f32[1024]{0:T(1024)S(1)}, f32[1024]{0:T(1024)S(1)}, /*index=5*/f...) all-reduce(f32[1024]{0:T(1024)S(1)} %get-tuple-element.183, ...), channel_id=2, replica_groups=mesh['dp'=8,'seq'=4] {'dp','seq'}, use_global_device_ids=true, to_apply=%region_16.17.clone | all-reduce | flops 12288 | bytes 98304
  729.2 95.5 %reduce-scatter.7.cloned.1.call-done = f32[32,1024]{1,0:T(8,128)} async-done(((f32[1024,1024]{1,0:T(8,128)}), f32[32,1024]{1,0:T(8,128)}) %reduce-scatter.7.cloned.1.call-update) | async-done | bytes 131088 | tf_op jit(solution)/shard_map/reduce_scatter | solution.py:240
  824.7 150.7 %reduce-scatter.9.cloned.1.call-done = f32[32,1024]{1,0:T(8,128)} async-done(((f32[1024,1024]{1,0:T(8,128)}), f32[32,1024]{1,0:T(8,128)}) %reduce-scatter.9.cloned.1.call-update) | async-done | bytes 131088 | tf_op jit(solution)/shard_map/reduce_scatter | solution.py:242
  975.4 151.4 %reduce-scatter.11.cloned.1.call-done = f32[32,1024]{1,0:T(8,128)} async-done(((f32[1024,1024]{1,0:T(8,128)}), f32[32,1024]{1,0:T(8,128)}) %reduce-scatter.11.cloned.1.call-update) | async-done | bytes 131088 | tf_op jit(solution)/shard_map/reduce_scatter | solution.py:243
  1126.8 362.0 %reduce-scatter.15.cloned.1.call-done = f32[32,4096]{1,0:T(8,128)} async-done(((f32[1024,4096]{1,0:T(8,128)}), f32[32,4096]{1,0:T(8,128)}) %reduce-scatter.15.cloned.1.call-update) | async-done | bytes 524304 | tf_op jit(solution)/shard_map/reduce_scatter | solution.py:249
  1488.8 364.7 %reduce-scatter.17.cloned.1.call-done = f32[128,1024]{1,0:T(8,128)} async-done(((f32[4096,1024]{1,0:T(8,128)}), f32[128,1024]{1,0:T(8,128)}) %reduce-scatter.17.cloned.1.call-update) | async-done | bytes 524304 | tf_op jit(solution)/shard_map/reduce_scatter | solution.py:251
  (237 shorter events, 47.1 us)
Async XLA Ops:
  7.2 8.7 copy-start.22
  7.2 9.4 copy-start.35
  7.2 9.4 copy-start.36
  7.2 9.5 copy-start.37
  7.2 9.5 copy-start.38
  7.2 9.5 copy-start.39
  7.3 9.5 copy-start.40
  7.3 9.5 copy-start.41
  7.3 9.5 copy-start.42
  7.3 9.5 copy-start.7
  7.3 63.8 %all-gather.12.cloned.1.call-start = ((), (), s32[]{:S(2)}) async-start(), calls=%async_computation.12 | async-start | bytes 2162688 | tf_op jit(solution)/shard_map/all_gather | solution.py:143
  9.1 120.8 %all-gather.10.cloned.1.call-start = ((), (), s32[]{:S(2)}) async-start(), calls=%async_computation.11 | async-start | bytes 2162688 | tf_op jit(solution)/shard_map/all_gather | solution.py:142
  10.7 178.0 %all-gather.8.cloned.1.call-start = ((), (), s32[]{:S(2)}) async-start(), calls=%async_computation.10 | async-start | bytes 2162688 | tf_op jit(solution)/shard_map/all_gather | solution.py:140
  12.3 381.1 %all-gather.14.cloned.1.call-start = ((), (), s32[]{:S(2)}) async-start(), calls=%async_computation.13 | async-start | bytes 2162688 | tf_op jit(solution)/shard_map/all_gather | solution.py:145
  13.9 382.8 %all-gather.16.cloned.1.call-start = ((), (), s32[]{:S(2)}) async-start(), calls=%async_computation.14 | async-start | bytes 8650752 | tf_op jit(solution)/shard_map/all_gather | solution.py:149
  15.8 432.0 %all-gather.18.cloned.1.call-start = ((), (), s32[]{:S(2)}) async-start(), calls=%async_computation.15 | async-start | bytes 8650752 | tf_op jit(solution)/shard_map/all_gather | solution.py:151
  17.1 57.2 %copy-start.2 = (f32[290,1024]{1,0:T(8,128)}, f32[290,1024]{1,0:T(8,128)S(1)}, u32[]{:S(2)}) copy-start(f32[290,1024]{1,0:T(8,128)S(1)} %reshape.308) | copy-start | bytes 3563524
  61.3 9.8 copy-start.26
  61.3 9.8 copy-start.24
  61.9 9.2 copy-start.16
  62.9 11.4 copy-start.18
  63.1 11.2 copy-start.28
  63.2 11.1 copy-start.30
  63.5 66.4 %copy-start.21 = (bf16[290,1024]{1,0:T(8,128)(2,1)}, bf16[290,1024]{1,0:T(8,128)(2,1)S(1)}, u32[]{:S(2)}) copy-start(bf16[290,1024]{1,0:T(8,128)(2,1)S(1)} %add_convert_fusion.2) | copy-start | bytes 1781764
  199.3 84.7 %all-to-all-start = ((bf16[2,145,3,1024]{1,0,2,3:T(2,128)(2,1)}), bf16[2,145,3,1024]{1,0,2,3:T(2,128)(2,1)S(1)}, u32[]{:S(2)}, u32[]{:S(2)}) async-start(bf16[2,145,3,1024]{1,0,2,3:T(2,128)(2,1)} %copy.101), calls=%async_computation | async-start | bytes 6291456 | tf_op jit(solution)/shard_map/all_to_all | solution.py:181
  288.0 5.4 copy-start.20
  288.0 5.4 copy-start.23
  303.2 5.4 copy-start.43
  304.4 87.5 %all-to-all-start.1 = ((bf16[2,580,256]{2,0,1:T(2,128)(2,1)}), bf16[2,580,256]{2,0,1:T(2,128)(2,1)S(1)}, u32[]{:S(2)}, u32[]{:S(2)}) async-start(bf16[2,580,256]{2,0,1:T(2,128)(2,1)} %copy.105), calls=%async_computation.1 | async-start | bytes 1187840 | tf_op jit(solution)/shard_map/all_to_all | solution.py:183
  396.4 84.1 %copy-start = (f32[290,1024]{1,0:T(8,128)}, f32[290,1024]{1,0:T(8,128)S(1)}, u32[]{:S(2)}) copy-start(f32[290,1024]{1,0:T(8,128)S(1)} %get-tuple-element.246) | copy-start | bytes 3563524
  474.0 6.5 copy-start.12
  474.0 6.5 copy-start.9
  480.6 2.0 copy-start.34
  481.0 1.0 copy-start.4
  484.4 8.0 copy-start.5
  488.0 44.5 %all-to-all-start.2 = ((bf16[2,145,1024]{1,0,2:T(2,128)(2,1)}), bf16[2,145,1024]{1,0,2:T(2,128)(2,1)}, u32[]{:S(2)}, u32[]{:S(2)}) async-start(bf16[2,145,1024]{1,0,2:T(2,128)(2,1)} %copy.109), calls=%async_computation.2 | async-start | bytes 2097152 | tf_op jit(solution)/shard_map/all_to_all | solution.py:215
  492.3 236.9 %reduce-scatter.13.cloned.1.call-start = ((), (), s32[]{:S(2)}) async-start(), calls=%async_computation.19 | async-start | bytes 4325376 | tf_op jit(solution)/shard_map/reduce_scatter | solution.py:245
  545.9 1.6 copy-start.14
  547.7 1.3 copy-start.15
  556.9 1.6 copy-start.14
  558.6 1.3 copy-start.15
  565.1 4.6 copy-start.8
  565.1 4.6 copy-start.17
  565.1 4.6 copy-start.19
  565.1 4.6 copy-start.25
  565.1 4.6 copy-start.27
  565.1 67.0 %all-to-all-start.3 = ((bf16[2,580,3,256]{3,0,2,1:T(2,128)(2,1)}), bf16[2,580,3,256]{3,0,2,1:T(2,128)(2,1)}, u32[]{:S(2)}, u32[]{:S(2)}) async-start(bf16[2,580,3,256]{3,0,2,1:T(2,128)(2,1)} %copy.114), calls=%async_computation.3 | async-start | bytes 3563520 | tf_op jit(solution)/shard_map/all_to_all | solution.py:217
  569.7 255.0 %reduce-scatter.7.cloned.1.call-start = ((), (), s32[]{:S(2)}) async-start(), calls=%async_computation.16 | async-start | bytes 4325376 | tf_op jit(solution)/shard_map/reduce_scatter | solution.py:240
  642.5 332.9 %reduce-scatter.9.cloned.1.call-start = ((), (), s32[]{:S(2)}) async-start(), calls=%async_computation.17 | async-start | bytes 4325376 | tf_op jit(solution)/shard_map/reduce_scatter | solution.py:242
  645.8 481.0 %reduce-scatter.11.cloned.1.call-start = ((), (), s32[]{:S(2)}) async-start(), calls=%async_computation.18 | async-start | bytes 4325376 | tf_op jit(solution)/shard_map/reduce_scatter | solution.py:243
  649.3 1.3 copy-start.1
  649.3 839.5 %reduce-scatter.15.cloned.1.call-start = ((), (), s32[]{:S(2)}) async-start(), calls=%async_computation.20 | async-start | bytes 17301504 | tf_op jit(solution)/shard_map/reduce_scatter | solution.py:249
  660.6 1.3 copy-start.10
  660.7 1192.9 %reduce-scatter.17.cloned.1.call-start = ((), (), s32[]{:S(2)}) async-start(), calls=%async_computation.21 | async-start | bytes 17301504 | tf_op jit(solution)/shard_map/reduce_scatter | solution.py:251
  672.9 1.1 copy-start.11
  675.4 2.6 copy-start.13
  678.0 1.3 copy-start.3
  678.0 1.3 copy-start.29
  678.0 1.3 copy-start.31
  678.0 2.0 copy-start.33
  680.0 1.3 copy-start.6
  681.8 1.8 copy-start.32
Sparse Core Ops, SparseCore 0:
  11.6 59.4 all-gather.11
  74.6 55.2 all-gather.9
  133.4 55.1 all-gather.7
  192.0 93.9 all-gather.13
  289.3 79.4 all-gather.15
  372.2 75.5 all-gather.17
  496.9 175.3 reduce-scatter.12
  675.1 149.5 reduce-scatter.6
  827.6 147.7 reduce-scatter.8
  978.1 148.6 reduce-scatter.10
  1129.7 359.1 reduce-scatter.14
  1491.6 361.9 reduce-scatter.16
where the time goes:
time: 1870 us; the launch traced here: 1860 us
  waiting for transfers between devices  1460 us (78%)
  blocking collectives  166 us (9%)
  matrix products  104 us (6%)
  local copies, waits for them, and re-layouts  69.7 us (4%)
  other arithmetic  25.2 us (1%)
    reduce_scatter x1, waiting for transfers between devices, per_device(): lax.psum_scatter(grad_down, ('dp', 'seq'), scatter_dimension=0, tiled=True)  365 us
    reduce_scatter x1, waiting for transfers between devices, per_device(): lax.psum_scatter(grad_up, ('dp', 'seq'), scatter_dimension=0, tiled=True)  362 us
    reduce_scatter x1, waiting for transfers between devices, per_device(): lax.psum_scatter(grad_value, ('dp', 'seq'), scatter_dimension=0, tiled=True)  151 us
    reduce_scatter x1, waiting for transfers between devices, per_device(): lax.psum_scatter(grad_key, ('dp', 'seq'), scatter_dimension=0, tiled=True)  151 us
    reduce_scatter x1, waiting for transfers between devices, per_device(): lax.psum_scatter(grad_query, ('dp', 'seq'), scatter_dimension=0, tiled=True)  95.5 us
    all_gather x1, blocking collectives, per_device(): lax.all_gather(b_up.astype(jnp.bfloat16), ('dp', 'seq'), axis=0, tiled=True)  83.2 us
    unnamed x2, blocking collectives  82.9 us
    all_to_all x1, waiting for transfers between devices, per_device(): lax.all_to_all(stacked, 'seq', split_axis=3, concat_axis=1, tiled=True)  80.4 us
  transfers between devices with their start and end apart: 16, of which 12 were waited for; matrix products, arithmetic and copies ran while one was open for 8% of the time, Pallas kernels for 0%

commit v1 on v0

--- a/solution.py
+++ b/solution.py
@@ -254,49 +254,326 @@
     return (block_out, input_grad) + tuple(every_shard)
 
 
+def swap_core(value):
+    return lax.ppermute(value, "core", [(0, 1), (1, 0)])
+
+
+def swap_x(value):
+    return lax.ppermute(value, "x", [(0, 1), (1, 0)])
+
+
+def swap_y(value):
+    return lax.ppermute(value, "y", [(0, 1), (1, 0)])
+
+
+def trade_z(value):
+    return lax.all_to_all(value, "z", split_axis=0, concat_axis=0, tiled=True)
+
+
+def in_order(index, mine, other, axis):
+    return jnp.where(
+        index == 0, jnp.stack([mine, other], axis=axis), jnp.stack([other, mine], axis=axis)
+    )
+
+
+def take(index, value, axis):
+    return lax.dynamic_index_in_dim(value, index, axis, keepdims=False)
+
+
+def gather_z(shard):
+    copies = lax.axis_size("z")
+    return trade_z(jnp.broadcast_to(shard[None], (copies,) + shard.shape))
+
+
+def gather_plane(rows):
+    here_x, here_y = (lax.axis_index("x"), lax.axis_index("y"))
+    half = rows.shape[0] // 2
+    first, second = (rows[:half], rows[half:])
+    first_x = swap_x(first)
+    second_y = swap_y(second)
+    first_pair = in_order(here_x, first, first_x, 0)
+    second_pair = in_order(here_y, second, second_y, 0)
+    first_y = swap_y(first_pair)
+    second_x = swap_x(second_pair)
+    first_all = in_order(here_y, first_pair, first_y, 0)
+    second_all = in_order(here_x, second_pair, second_x, 1)
+    return jnp.stack([first_all, second_all], axis=2).reshape(4 * rows.shape[0], rows.shape[1])
+
+
+def scatter_plane(total):
+    here_x, here_y = (lax.axis_index("x"), lax.axis_index("y"))
+    rows = total.shape[0] // 4
+    half = rows // 2
+    blocks = total.reshape(2, 2, 2, half, total.shape[1])
+    first, second = (blocks[:, :, 0], blocks[:, :, 1])
+    first_got = swap_y(take(1 - here_y, first, 0).astype(jnp.bfloat16))
+    second_got = swap_x(take(1 - here_x, second, 1).astype(jnp.bfloat16))
+    first_sum = take(here_y, first, 0) + first_got
+    second_sum = take(here_x, second, 1) + second_got
+    first_last = swap_x(take(1 - here_x, first_sum, 0).astype(jnp.bfloat16))
+    second_last = swap_y(take(1 - here_y, second_sum, 0).astype(jnp.bfloat16))
+    return jnp.concatenate(
+        [
+            take(here_x, first_sum, 0) + first_last,
+            take(here_y, second_sum, 0) + second_last,
+        ],
+        axis=0,
+    )
+
+
+def scatter_z(parts):
+    return jnp.sum(trade_z(parts.astype(jnp.bfloat16)).astype(jnp.float32), axis=0)
+
+
+def own_image(
+    tokens_in,
+    cotangent,
+    group_count,
+    key_mask,
+    ln1_gain,
+    ln1_shift,
+    w_query,
+    b_query,
+    w_key,
+    w_value,
+    b_value,
+    w_out,
+    b_out,
+    ln2_gain,
+    ln2_shift,
+    w_up,
+    b_up,
+    w_down,
+    b_down,
+):
+    low = jnp.bfloat16
+    slot_count, tok_dev, width = tokens_in.shape
+    core, place = (lax.axis_index("core"), lax.axis_index("z"))
+    depth = lax.axis_size("z")
+    planes = lax.axis_size("y") * lax.axis_size("x")
+    length = depth * tok_dev
+    block = width // (2 * planes)
+    part_rows = w_query.shape[0]
+    half = width // 2
+    ff_width = w_up.shape[1]
+    ff_half = ff_width // 2
+    ff_block = ff_width // (2 * planes)
+    ff_rows = w_down.shape[0]
+
+    def split_cols(value, size):
+        lead = value.shape[:-1]
+        view = value.reshape(lead + (-1, 2, size))
+        even, odd = (view[..., 0, :], view[..., 1, :])
+        mine = jnp.where(core == 0, even, odd)
+        other = jnp.where(core == 0, odd, even)
+        return (mine.reshape(lead + (-1,)), other.reshape(lead + (-1,)))
+
+    def join_cols(mine, other, size):
+        lead = mine.shape[:-1]
+        view = lead + (-1, size)
+        return in_order(core, mine.reshape(view), other.reshape(view), len(lead) + 1).reshape(
+            lead + (-1,)
+        )
+
+    def to_image(local):
+        mine, other = split_cols(local, block)
+        images = in_order(core, mine, swap_core(other), 0)
+        images = images.reshape(2 * slot_count, tok_dev, half)
+        mine = trade_z(images).reshape(length, half)
+        return join_cols(mine, swap_core(mine), block)
+
+    def to_tokens(mine):
+        images = trade_z(mine.reshape(depth, tok_dev, half))
+        images = images.reshape(2, slot_count, tok_dev, half)
+        other = swap_core(take(1 - core, images, 0))
+        return join_cols(take(core, images, 0), other, block)
+
+    vectors = (ln1_gain, ln1_shift, b_query, b_value, b_out, ln2_gain, ln2_shift, b_down)
+    small = jnp.concatenate([vector.astype(low) for vector in vectors] + [b_up.astype(low)])
+    small_rows = jnp.pad(small, (0, part_rows * 128 - small.shape[0])).reshape(part_rows, 128)
+
+    project = gather_z(
+        jnp.concatenate(
+            [w_query.astype(low), w_key.astype(low), w_value.astype(low), small_rows], axis=1
+        )
+    )
+    image_in = to_image(tokens_in)
+    mine, other = split_cols(project[..., : 3 * width], block)
+    small_part = project[..., 3 * width :]
+    project_pair = in_order(
+        core,
+        jnp.concatenate([mine, small_part], axis=-1),
+        swap_core(jnp.concatenate([other, small_part], axis=-1)),
+        0,
+    )
+    project_all = gather_plane(project_pair.reshape(2 * depth * part_rows, 3 * half + 128))
+    qkv_w = project_all[:, : 3 * half]
+    small_all = project_all[:, 3 * half :].reshape(-1, part_rows * 128)[:, : small.shape[0]]
+    small_all = small_all.astype(jnp.float32)
+    count = len(vectors)
+    wide = small_all[:, : count * part_rows].reshape(-1, count, part_rows)
+    wide = wide.transpose(1, 0, 2).reshape(count, width)
+    gain_one, shift_one, query_b, value_b, out_b, gain_two, shift_two, down_b = [
+        wide[index] for index in range(count)
+    ]
+    query_b = split_cols(query_b, block)[0]
+    value_b = split_cols(value_b, block)[0]
+    up_b = split_cols(small_all[:, count * part_rows :].reshape(ff_width), ff_block)[0]
+
+    out_mine = gather_plane(gather_z(w_out.astype(low)).reshape(depth * part_rows, width))
+    out_other = swap_core(out_mine)
+
+    up_part = gather_z(w_up.astype(low))
+    mine, other = split_cols(up_part, ff_block)
+    up_pair = in_order(core, mine, swap_core(other), 0)
+    up_w = gather_plane(up_pair.reshape(2 * depth * part_rows, ff_half))
+    down_w = gather_plane(gather_z(w_down.astype(low)).reshape(depth * ff_rows, width))
+
+    live_slot = jnp.arange(slot_count) < group_count[0]
+    live_low = live_slot.astype(low)[:, None, None]
+    upstream_low = to_image(cotangent * live_low)
+
+    owner, slot = (place // slot_count, place % slot_count)
+    mask_mine = take(slot, key_mask, 0).astype(jnp.float32)[None, :]
+    key_keep = jnp.where(core == owner, mask_mine, swap_core(mask_mine))[0]
+
+    inputs = image_in.astype(jnp.float32)
+    normal_one, inverse_one = norm_stats(inputs)
+    normed_one = (normal_one * gain_one + shift_one).astype(low)
+    qkv_b = jnp.concatenate([query_b, jnp.zeros_like(query_b), value_b])
+    stacked = (product(normed_one, qkv_w) + qkv_b).astype(low).reshape(length, 3, half)
+    mixed, log_total = attend_image((stacked, key_keep))
+    mixed_other = swap_core(mixed)
+    middle = inputs + (product(mixed, out_mine) + product(mixed_other, out_other)) + out_b
+    normal_two, inverse_two = norm_stats(middle)
+    normed_two = (normal_two * gain_two + shift_two).astype(low)
+    hidden = product(normed_two, up_w) + up_b
+    gate_sig = jax.nn.sigmoid(SLOPE * hidden)
+    activated = (hidden * gate_sig).astype(low)
+    grad_down = contract_rows(activated, upstream_low)
+    grad_act = contract_cols(upstream_low, down_w)
+    grad_hidden = (grad_act * (gate_sig + SLOPE * hidden * gate_sig * (1.0 - gate_sig))).astype(low)
+    grad_two = contract_cols(grad_hidden, up_w)
+    grad_normed_two = grad_two + swap_core(grad_two)
+    grad_up = contract_rows(normed_two, grad_hidden)
+
+    result = product(activated, down_w)
+    mine, other = split_cols(result, block)
+    result = split_cols(middle + down_b, block)[0] + (mine + swap_core(other))
+    block_out = to_tokens(result.astype(low)) * live_low
+
+    upstream = upstream_low.astype(jnp.float32)
+    grad_mid, grad_gain_two, grad_shift_two = norm_back(
+        grad_normed_two, normal_two, inverse_two, gain_two
+    )
+    grad_middle = upstream + grad_mid
+    branch_low = grad_middle.astype(low)
+    grad_mixed = contract_cols(branch_low, out_mine).astype(low)
+    grad_out = contract_rows(mixed, branch_low)
+    grad_stacked = attend_back((stacked, grad_mixed, log_total, key_keep))
+    grad_qkv = grad_stacked.reshape(length, 3 * half)
+    grad_project = contract_rows(normed_one, grad_qkv)
+
+    grad_one = contract_cols(grad_qkv, qkv_w)
+    scaled = grad_one * gain_one
+    sums = jnp.concatenate(
+        [
+            jnp.sum(scaled, axis=1, keepdims=True),
+            jnp.sum(scaled * normal_one, axis=1, keepdims=True),
+        ],
+        axis=1,
+    )
+    mine, other = split_cols(grad_one, block)
+    got = swap_core(jnp.concatenate([other, jnp.pad(sums, ((0, 0), (0, 126)))], axis=1))
+    grad_normed_one = mine + got[:, :half]
+    means = (sums + got[:, half : half + 2]) / width
+    normal_mine = split_cols(normal_one, block)[0]
+    grad_first = inverse_one * (
+        grad_normed_one * split_cols(gain_one, block)[0]
+        - means[:, :1]
+        - normal_mine * means[:, 1:]
+    )
+    input_grad = to_tokens((split_cols(grad_middle, block)[0] + grad_first).astype(low))
+
+    grad_gain_one = jnp.sum(grad_normed_one * normal_mine, axis=0)
+    grad_shift_one = jnp.sum(grad_normed_one, axis=0)
+    bias_qkv = jnp.sum(grad_qkv.astype(jnp.float32), axis=0)
+    small_grads = (
+        grad_gain_one,
+        grad_shift_one,
+        bias_qkv[:half],
+        bias_qkv[2 * half :],
+        split_cols(jnp.sum(branch_low.astype(jnp.float32), axis=0), block)[0],
+        split_cols(grad_gain_two, block)[0],
+        split_cols(grad_shift_two, block)[0],
+        split_cols(jnp.sum(upstream, axis=0), block)[0],
+    )
+    small_wide = jnp.stack(small_grads).reshape(count, planes * depth, part_rows)
+    small_wide = small_wide.transpose(1, 0, 2).reshape(planes * depth, count * part_rows)
+    grad_up_b = jnp.sum(grad_hidden.astype(jnp.float32), axis=0)
+    small_wide = jnp.concatenate([small_wide, grad_up_b.reshape(planes * depth, -1)], axis=1)
+    small_wide = jnp.pad(small_wide, ((0, 0), (0, part_rows * 128 - small.shape[0])))
+    small_wide = jnp.broadcast_to(
+        small_wide.reshape(planes, 1, depth * part_rows, 128),
+        (planes, 2, depth * part_rows, 128),
+    ).reshape(width, 128)
+
+    down_rows = scatter_z(scatter_plane(grad_down).reshape(depth, ff_rows, width))
+
+    def own_rows(total, cols, size):
+        by_z = scatter_plane(total).reshape(2, depth, part_rows, cols).transpose(1, 0, 2, 3)
+        pair = scatter_z(by_z)
+        mine, other = (take(core, pair, 0), swap_core(take(1 - core, pair, 0)))
+        return (mine, other)
+
+    mine, other = own_rows(grad_up, ff_half, ff_block)
+    up_rows = join_cols(mine, other, ff_block)
+    out_rows = scatter_z(scatter_plane(grad_out).reshape(depth, part_rows, width))
+    mine, other = own_rows(
+        jnp.concatenate([grad_project, small_wide], axis=1), 3 * half + 128, block
+    )
+    project_rows = join_cols(mine[:, : 3 * half], other[:, : 3 * half], block)
+    small_out = mine[:, 3 * half :].reshape(-1)[: small.shape[0]]
+    pieces = [small_out[k * part_rows : (k + 1) * part_rows] for k in range(count)]
+    return (
+        block_out,
+        input_grad,
+        pieces[0],
+        pieces[1],
+        project_rows[:, :width],
+        pieces[2],
+        project_rows[:, width : 2 * width],
+        project_rows[:, 2 * width :],
+        pieces[3],
+        out_rows,
+        pieces[4],
+        pieces[5],
+        pieces[6],
+        up_rows,
+        small_out[count * part_rows :],
+        down_rows,
+        pieces[7],
+    )
+
+
 def solution(mesh):
+    dp, seq = (mesh.shape["dp"], mesh.shape["seq"])
+    function, axes, by_image, by_part = (per_device, mesh, "dp", ("dp", "seq"))
+    by_token = "seq"
+    if dp == 8 and seq == 4:
+        function = own_image
+        axes = jax.sharding.Mesh(mesh.devices.reshape(2, 2, 2, seq), ("y", "x", "core", "z"))
+        by_image, by_token = (("y", "x", "core"), "z")
+        by_part = ("y", "x", "core", "z")
+    tokens, vector, matrix = (P(by_image, by_token, None), P(by_part), P(by_part, None))
+    params = (
+        (vector, vector, matrix, vector, matrix, matrix, vector, matrix)
+        + (vector, vector, vector, matrix, vector, matrix, vector)
+    )
     return jax.shard_map(
-        per_device,
-        mesh=mesh,
-        in_specs=(
-            P("dp", "seq", None),
-            P("dp", "seq", None),
-            P("dp"),
-            P("dp", None),
-            P(("dp", "seq")),
-            P(("dp", "seq")),
-            P(("dp", "seq"), None),
-            P(("dp", "seq")),
-            P(("dp", "seq"), None),
-            P(("dp", "seq"), None),
-            P(("dp", "seq")),
-            P(("dp", "seq"), None),
-            P(("dp", "seq")),
-            P(("dp", "seq")),
-            P(("dp", "seq")),
-            P(("dp", "seq"), None),
-            P(("dp", "seq")),
-            P(("dp", "seq"), None),
-            P(("dp", "seq")),
-        ),
-        out_specs=(
-            P("dp", "seq", None),
-            P("dp", "seq", None),
-            P(("dp", "seq")),
-            P(("dp", "seq")),
-            P(("dp", "seq"), None),
-            P(("dp", "seq")),
-            P(("dp", "seq"), None),
-            P(("dp", "seq"), None),
-            P(("dp", "seq")),
-            P(("dp", "seq"), None),
-            P(("dp", "seq")),
-            P(("dp", "seq")),
-            P(("dp", "seq")),
-            P(("dp", "seq"), None),
-            P(("dp", "seq")),
-            P(("dp", "seq"), None),
-            P(("dp", "seq")),
-        ),
+        function,
+        mesh=axes,
+        in_specs=(tokens, tokens, P(by_image), P(by_image, None)) + params,
+        out_specs=(tokens, tokens) + params,
         check_vma=False,
     )

time: 1870 us -> 647 us (0.35)
  waiting for transfers between devices: 1460 us -> 175 us
  blocking collectives: 166 us -> 0 us
  local copies, waits for them, and re-layouts: 69.7 us -> 173 us
  other arithmetic: 25.2 us -> 125 us
  starting transfers between devices: 17 us -> 85 us
  matrix products: 104 us -> 75.6 us
    reduce_scatter x6 -> x0, waiting for transfers between devices: 1120 us -> none  [the longest x1 365 us: per_device(): lax.psum_scatter(grad_down, ('dp', 'seq'), scatter_dimension=0, tiled=True)]
    all_gather x6 -> x0, waiting for transfers between devices: 160 us -> none  [the longest x1 56.2 us: per_device(): lax.all_gather(w_query.astype(jnp.bfloat16), ('dp', 'seq'), axis=0, tiled...]
    all_gather x1 -> x0, blocking collectives: 83.2 us -> none  [per_device(): lax.all_gather(b_up.astype(jnp.bfloat16), ('dp', 'seq'), axis=0, tiled=True)]
    unnamed x2 -> x0, blocking collectives: 82.9 us -> none
    all_to_all x4 -> x12, waiting for transfers between devices: 177 us -> 111 us  [trade_z(): return lax.all_to_all(value, 'z', split_axis=0, concat_axis=0, tiled=True)]
    ppermute x0 -> x48, waiting for transfers between devices: none -> 64.8 us  [the longest x16 43.6 us: swap_x(): return lax.ppermute(value, 'x', [(0, 1), (1, 0)])]
    select_n x0 -> x39, other arithmetic: none -> 52.2 us  [the longest x24 28.1 us: in_order(): jnp.where(index == 0, jnp.stack([mine, other], axis=axis), jnp.stack([oth...]
    ppermute x0 -> x48, starting transfers between devices: none -> 36.6 us  [the longest x16 17.8 us: swap_x(): return lax.ppermute(value, 'x', [(0, 1), (1, 0)])]
  transfers between devices with their start and end apart: 16 -> 60, of which waited for: 12 -> 24; matrix products, arithmetic and copies ran while one was open for 8% -> 48% of each run, Pallas kernels for 0% -> 0%
where the time goes in v1:
time: 647 us; the launch traced here: 638 us
  waiting for transfers between devices  175 us (27%)
  local copies, waits for them, and re-layouts  173 us (27%)
  other arithmetic  125 us (19%)
  starting transfers between devices  85 us (13%)
  matrix products  75.6 us (12%)
    all_to_all x12, waiting for transfers between devices, trade_z(): return lax.all_to_all(value, 'z', split_axis=0, concat_axis=0, tiled=True)  111 us
    all_to_all x12, starting transfers between devices, trade_z(): return lax.all_to_all(value, 'z', split_axis=0, concat_axis=0, tiled=True)  48.4 us
    ppermute x16, waiting for transfers between devices, swap_x(): return lax.ppermute(value, 'x', [(0, 1), (1, 0)])  43.6 us
    unnamed x198, local copies, waits for them, and re-layouts  31.3 us
    select_n x24, other arithmetic, in_order(): jnp.where(index == 0, jnp.stack([mine, other], axis=axis), jnp.stack([oth...  28.1 us
    select_n x14, other arithmetic, split_cols(): mine = jnp.where(core == 0, even, odd)  22.3 us
    dot_general x5, matrix products, product(): return jnp.dot(left, right, preferred_element_type=jnp.float32)  20.9 us
    dot_general x4, matrix products, contract_rows(): lax.dot_general(left, right, (((0,), (0,)), ((), ())), preferred_element_...  19.4 us
  transfers between devices with their start and end apart: 60, of which 24 were waited for; matrix products, arithmetic and copies ran while one was open for 48% of the time, Pallas kernels for 0%

profile of v1, /device:TPU:0, one launch (start us, length us, event | category | flops | bytes accessed | tf_op | source)
XLA Modules:
  0.0 638.2 jit_solution(1449853699407298064)
XLA Ops:
  4.1 3.8 fusion.52
  9.3 5.9 all-to-all-start.2
  17.0 7.7 %all-to-all-done.2 = bf16[4,32,1024]{2,1,0:T(8,128)(2,1)S(1)} async-done(((bf16[4,32,1024]{2,1,0:T(8,128)(2,1)}), bf16[4,32,1024]{2,1,0:T(8,128)(2,1)S(1)}, u32[]{:S(2)}, u32[]{:S(2)}) %all-to-all-start.2) | async-done | bytes 262176 | tf_op jit(solution)/shard_map/all_to_all | solution.py:270
  24.7 3.7 all-to-all-start
  29.1 3.8 fusion.54
  35.6 7.9 %all-to-all-done = bf16[4,145,512]{2,1,0:T(8,128)(2,1)S(1)} async-done(((bf16[4,145,512]{2,1,0:T(8,128)(2,1)}), bf16[4,145,512]{2,1,0:T(8,128)(2,1)S(1)}, u32[]{:S(2)}, u32[]{:S(2)}) %all-to-all-start) | async-done | bytes 593952 | tf_op jit(solution)/shard_map/all_to_all | solution.py:270
  43.6 3.5 all-to-all-start.6
  47.5 15.6 %all-to-all-done.6 = bf16[4,145,512]{2,1,0:T(8,128)(2,1)S(1)} async-done(((bf16[4,145,512]{2,1,0:T(8,128)(2,1)}), bf16[4,145,512]{2,1,0:T(8,128)(2,1)S(1)}, u32[]{:S(2)}, u32[]{:S(2)}) %all-to-all-start.6) | async-done | bytes 593952 | tf_op jit(solution)/shard_map/all_to_all | solution.py:270
  64.0 3.5 all-to-all-start.1
  68.6 19.2 %all-to-all-done.1 = bf16[4,32,3200]{2,1,0:T(8,128)(2,1)S(1)} async-done(((bf16[4,32,3200]{2,1,0:T(8,128)(2,1)}), bf16[4,32,3200]{2,1,0:T(8,128)(2,1)S(1)}, u32[]{:S(2)}, u32[]{:S(2)}) %all-to-all-start.1) | async-done | bytes 819232 | tf_op jit(solution)/shard_map/all_to_all | solution.py:270
  89.2 3.5 all-to-all-start.4
  103.3 14.7 %all-to-all-done.4 = bf16[4,128,1024]{2,1,0:T(8,128)(2,1)S(1)} async-done(((bf16[4,128,1024]{2,1,0:T(8,128)(2,1)}), bf16[4,128,1024]{2,1,0:T(8,128)(2,1)S(1)}, u32[]{:S(2)}, u32[]{:S(2)}) %all-to-all-start.4) | async-done | bytes 1048608 | tf_op jit(solution)/shard_map/all_to_all | solution.py:270
  119.1 4.5 all-to-all-start.3
  144.2 4.8 all-to-all-done.3
  150.8 5.6 fusion.32
  183.7 3.5 reshape.2100
  197.4 2.8 fusion.40
  204.4 2.8 fusion.41
  207.2 2.8 maximum_select_fusion.16
  210.0 11.6 %collective-permute-done.15 = bf16[128,2048]{1,0:T(8,128)(2,1)S(1)} collective-permute-done((bf16[128,2048]{1,0:T(8,128)(2,1)S(1)}, bf16[128,2048]{1,0:T(8,128)(2,1)S(1)}, u32[]{:S(2)}, u32[]{:S(2)}) %collective-permute-start.15) | collective-permute-done | bytes 524320 | tf_op jit(solution)/shard_map/ppermute | solution.py:262
  239.2 3.0 slice_reduce_fusion.3
  250.6 5.5 add_convert_fusion
  256.0 2.7 copy.367
  280.1 6.6 %copy.380 = bf16[1024,2048]{1,0:T(8,128)(2,1)} copy(bf16[1024,2048]{0,1:T(8,128)(2,1)} %bitcast.391) | data formatting | bytes 8388608 | tf_op jit(solution)/shard_map/dot_general | solution.py:31
  286.6 3.8 fusion.102
  296.2 5.0 fusion.10
  301.2 4.8 convert_reduce_fusion
  306.0 4.1 fusion.104
  310.1 6.1 fusion.82
  316.2 4.3 fusion.15
  320.5 6.7 %dot_general.96 = bf16[2,2,2,256,580]{3,2,1,0,4:T(2,128)(2,1)} reshape(bf16[2048,580]{0,1:T(8,128)(2,1)} %get-tuple-element.201) | data formatting | bytes 4751360 | tf_op jit(solution)/shard_map/dot_general | solution.py:35
  332.8 4.0 fusion.87
  340.2 6.1 fusion.17
  346.3 4.3 fusion.86
  351.5 11.6 %collective-permute-done.41 = bf16[2,128,2048]{2,1,0:T(8,128)(2,1)S(1)} collective-permute-done((bf16[2,128,2048]{2,1,0:T(8,128)(2,1)S(1)}, bf16[2,128,2048]{2,1,0:T(8,128)(2,1)S(1)}, u32[]{:S(2)}, u32[]{:S(2)}) %collective-permute-start.41) | collective-permute-done | bytes 1048608 | tf_op jit(solution)/shard_map/ppermute | solution.py:262
  369.5 15.5 %collective-permute-done.46 = bf16[2,256,1024]{2,1,0:T(8,128)(2,1)S(1)} collective-permute-done((bf16[2,256,1024]{2,1,0:T(8,128)(2,1)S(1)}, bf16[2,256,1024]{2,1,0:T(8,128)(2,1)S(1)}, u32[]{:S(2)}, u32[]{:S(2)}) %collective-permute-start.46) | collective-permute-done | bytes 1048608 | tf_op jit(solution)/shard_map/ppermute | solution.py:262
  392.0 9.3 %collective-permute-done.42 = bf16[128,2048]{1,0:T(8,128)(2,1)S(1)} collective-permute-done((bf16[128,2048]{1,0:T(8,128)(2,1)S(1)}, bf16[128,2048]{1,0:T(8,128)(2,1)S(1)}, u32[]{:S(2)}, u32[]{:S(2)}) %collective-permute-start.42) | collective-permute-done | bytes 524320 | tf_op jit(solution)/shard_map/ppermute | solution.py:266
  404.3 4.2 all-to-all-start.10
  414.6 3.7 multiply_reduce_fusion.1
  422.9 4.3 reshape.2089
  427.5 6.4 %fusion.2 = bf16[8,64,580]{2,1,0:T(8,128)(2,1)S(1)} fusion(bf16[580,8,64]{0,2,1:T(8,128)(2,1)S(1)} %bitcast.403, f32[8,580,580]{1,2,0:T(8,128)} %copy-done, f32[8,580]{1,0:T(8,128)S(1)} %log_add_fusion), kind=kOutput, calls=%fused_computation.10 | convolution fusion | flops 349856000 | bytes 11971200 | tf_op jit(solution)/shard_map/hqk,qhd->khd/dot_general | solution.py:86
  433.9 8.3 %multiply_reduce_fusion = (f32[8,580]{1,0:T(8,128)S(1)}, f32[8,580,580]{1,2,0:T(8,128)}) fusion(f32[8,580,580]{1,2,0:T(8,128)} %copy-done, f32[8,580]{1,0:T(8,128)S(1)} %log_add_fusion, bf16[580,8,64]{0,2,1:T(8,128)(2,1)S(1)} %bitcast.404, bf16[580,8,64]{0,2,1:T(8,128)(2,1)S(1)} %bitcast.441), kind=kOutput, calls=%fused_computation.1 | convolution fusion | flops 352542560 | bytes 22754560 | tf_op jit(solution)/shard_map/qhd,khd->hqk/dot_general | solution.py:92
  442.3 6.3 multiply_convert_fusion
  460.2 4.8 reshape.2091
  466.7 3.3 fusion.89
  474.0 3.4 reshape.2081
  477.4 4.4 fusion.90
  484.5 3.2 fusion.88
  488.6 3.4 copy_select_fusion.3
  495.4 2.8 select_maximum_fusion
  498.3 6.3 fusion.30
  522.6 2.7 collective-permute-done.38
  530.2 4.2 all-to-all-start.11
  534.5 4.0 fusion.81
  551.7 8.3 %all-to-all-done.11 = bf16[4,128,1024]{2,1,0:T(8,128)(2,1)} async-done(((bf16[4,128,1024]{2,1,0:T(8,128)(2,1)}), bf16[4,128,1024]{2,1,0:T(8,128)(2,1)}, u32[]{:S(2)}, u32[]{:S(2)}) %all-to-all-start.11) | async-done | bytes 1048608 | tf_op jit(solution)/shard_map/all_to_all | solution.py:270
  560.0 4.0 all-to-all-start.9
  564.1 3.2 fusion.25
  567.3 5.3 all-to-all-done.9
  572.6 4.2 all-to-all-start.5
  582.4 8.9 %all-to-all-done.5 = bf16[4,145,512]{2,1,0:T(8,128)(2,1)} async-done(((bf16[4,145,512]{2,1,0:T(8,128)(2,1)}), bf16[4,145,512]{2,1,0:T(8,128)(2,1)}, u32[]{:S(2)}, u32[]{:S(2)}) %all-to-all-start.5) | async-done | bytes 593952 | tf_op jit(solution)/shard_map/all_to_all | solution.py:270
  591.3 3.5 all-to-all-start.7
  597.4 12.3 %all-to-all-done.7 = bf16[4,145,512]{2,1,0:T(8,128)(2,1)S(1)} async-done(((bf16[4,145,512]{2,1,0:T(8,128)(2,1)}), bf16[4,145,512]{2,1,0:T(8,128)(2,1)S(1)}, u32[]{:S(2)}, u32[]{:S(2)}) %all-to-all-start.7) | async-done | bytes 593952 | tf_op jit(solution)/shard_map/all_to_all | solution.py:270
  609.7 3.7 all-to-all-start.8
  628.4 5.8 all-to-all-done.8
  (545 shorter events, 264.5 us)
Async XLA Ops:
  7.9 20.5 %copy-start.55 = (bf16[2,145,1024]{2,0,1:T(2,128)(2,1)S(1)}, bf16[2,145,1024]{2,0,1:T(2,128)(2,1)}, u32[]{:S(2)}) copy-start(bf16[2,145,1024]{2,0,1:T(2,128)(2,1)} %param.20) | copy-start | bytes 1781764
  8.0 8.0 %collective-permute-start = (bf16[2,145,512]{2,1,0:T(8,128)(2,1)S(1)}, bf16[2,145,512]{2,1,0:T(8,128)(2,1)S(1)}, u32[]{:S(2)}, u32[]{:S(2)}) collective-permute-start(bf16[2,145,512]{2,1,0:T(8,128)(2,1)S(1)} %select_n.804), channel_id=1, source_target_pairs={{0,4},{4,0},{1,5},{5,1},{2,6},{6,2},{3,7},{7,3},{8,12},{12,8},{9,1... | collective-permute-start | bytes 890888 | tf_op jit(solution)/shard_map/ppermute | solution.py:258
  9.3 15.4 %all-to-all-start.2 = ((bf16[4,32,1024]{2,1,0:T(8,128)(2,1)}), bf16[4,32,1024]{2,1,0:T(8,128)(2,1)S(1)}, u32[]{:S(2)}, u32[]{:S(2)}) async-start(bf16[4,32,1024]{2,1,0:T(8,128)(2,1)} %broadcast_in_dim.38), calls=%async_computation.2 | async-start | bytes 524288 | tf_op jit(solution)/shard_map/all_to_all | solution.py:270
  24.7 18.8 %all-to-all-start = ((bf16[4,145,512]{2,1,0:T(8,128)(2,1)}), bf16[4,145,512]{2,1,0:T(8,128)(2,1)S(1)}, u32[]{:S(2)}, u32[]{:S(2)}) async-start(bf16[4,145,512]{2,1,0:T(8,128)(2,1)} %bitcast.1), calls=%async_computation | async-start | bytes 1245184 | tf_op jit(solution)/shard_map/all_to_all | solution.py:270
  29.1 18.2 %copy-start.57 = (f32[32,1024]{1,0:T(8,128)S(1)}, f32[32,1024]{1,0:T(8,128)}, u32[]{:S(2)}) copy-start(f32[32,1024]{1,0:T(8,128)} %param.25) | copy-start | bytes 393220
  33.0 1.7 collective-permute-start.25
  43.6 19.5 %all-to-all-start.6 = ((bf16[4,145,512]{2,1,0:T(8,128)(2,1)}), bf16[4,145,512]{2,1,0:T(8,128)(2,1)S(1)}, u32[]{:S(2)}, u32[]{:S(2)}) async-start(bf16[4,145,512]{2,1,0:T(8,128)(2,1)} %bitcast.91), calls=%async_computation.6 | async-start | bytes 1245184 | tf_op jit(solution)/shard_map/all_to_all | solution.py:270
  64.0 23.8 %all-to-all-start.1 = ((bf16[4,32,3200]{2,1,0:T(8,128)(2,1)}), bf16[4,32,3200]{2,1,0:T(8,128)(2,1)S(1)}, u32[]{:S(2)}, u32[]{:S(2)}) async-start(bf16[4,32,3200]{2,1,0:T(8,128)(2,1)} %broadcast_in_dim.34), calls=%async_computation.1 | async-start | bytes 1638400 | tf_op jit(solution)/shard_map/all_to_all | solution.py:270
  67.5 26.8 %copy-start.72 = (s32[2,580]{1,0:T(2,128)S(1)}, s32[2,580]{1,0:T(2,128)}, u32[]{:S(2)}) copy-start(s32[2,580]{1,0:T(2,128)} %param.22) | copy-start | bytes 13924
  89.2 28.8 %all-to-all-start.4 = ((bf16[4,128,1024]{2,1,0:T(8,128)(2,1)}), bf16[4,128,1024]{2,1,0:T(8,128)(2,1)S(1)}, u32[]{:S(2)}, u32[]{:S(2)}) async-start(bf16[4,128,1024]{2,1,0:T(8,128)(2,1)} %broadcast_in_dim.40), calls=%async_computation.4 | async-start | bytes 2097152 | tf_op jit(solution)/shard_map/all_to_all | solution.py:270
  92.8 5.0 collective-permute-start.10
  94.4 2.7 collective-permute-start.7
  95.5 6.4 %collective-permute-start.8 = (bf16[64,1024]{1,0:T(8,128)(2,1)S(1)}, bf16[64,1024]{1,0:T(8,128)(2,1)S(1)}, u32[]{:S(2)}, u32[]{:S(2)}) collective-permute-start(bf16[64,1024]{1,0:T(8,128)(2,1)S(1)} %bitcast.454), channel_id=1, source_target_pairs={{0,8},{8,0},{1,9},{9,1},{2,10},{10,2},{3,11},{11,3},{4,12},{12,4},... | collective-permute-start | bytes 393224 | tf_op jit(solution)/shard_map/ppermute | solution.py:262
  97.8 25.9 %collective-permute-start.11 = (bf16[2,64,1024]{2,1,0:T(8,128)(2,1)S(1)}, bf16[2,64,1024]{2,1,0:T(8,128)(2,1)}, u32[]{:S(2)}, u32[]{:S(2)}) collective-permute-start(bf16[2,64,1024]{2,1,0:T(8,128)(2,1)S(1)} %maximum_select_fusion.33), channel_id=1, source_target_pairs={{0,8},{8,0},{1,9},{9,1},{2,10},{10,2},{3,11},{11,3},{4,12},{12,4},... | collective-permute-start | bytes 786440 | tf_op jit(solution)/shard_map/ppermute | solution.py:262
  102.7 22.1 %collective-permute-start.9 = (bf16[2,64,1024]{2,1,0:T(8,128)(2,1)}, bf16[2,64,1024]{2,1,0:T(8,128)(2,1)}, u32[]{:S(2)}, u32[]{:S(2)}) collective-permute-start(bf16[2,64,1024]{2,1,0:T(8,128)(2,1)} %maximum_select_fusion.31), channel_id=1, source_target_pairs={{0,16},{16,0},{1,17},{17,1},{2,18},{18,2},{3,19},{19,3},{4,20},{20... | collective-permute-start | bytes 786440 | tf_op jit(solution)/shard_map/ppermute | solution.py:266
  119.1 29.8 %all-to-all-start.3 = ((bf16[4,32,4096]{2,1,0:T(8,128)(2,1)}), bf16[4,32,4096]{2,1,0:T(8,128)(2,1)}, u32[]{:S(2)}, u32[]{:S(2)}) async-start(bf16[4,32,4096]{2,1,0:T(8,128)(2,1)} %broadcast_in_dim.39), calls=%async_computation.3 | async-start | bytes 2097152 | tf_op jit(solution)/shard_map/all_to_all | solution.py:270
  126.0 160.6 %collective-permute-start.13 = (bf16[512,1024]{1,0:T(8,128)(2,1)S(1)}, bf16[512,1024]{1,0:T(8,128)(2,1)}, u32[]{:S(2)}, u32[]{:S(2)}) collective-permute-start(bf16[512,1024]{1,0:T(8,128)(2,1)S(1)} %bitcast.393), channel_id=1, source_target_pairs={{0,4},{4,0},{1,5},{5,1},{2,6},{6,2},{3,7},{7,3},{8,12},{12,8},{9,1... | collective-permute-start | bytes 3145736 | tf_op jit(solution)/shard_map/ppermute | solution.py:258
  129.3 34.5 %collective-permute-start.1 = (bf16[580,512]{1,0:T(8,128)(2,1)}, bf16[580,512]{1,0:T(8,128)(2,1)}, u32[]{:S(2)}, u32[]{:S(2)}) collective-permute-start(bf16[580,512]{1,0:T(8,128)(2,1)} %reshape.2073), channel_id=1, source_target_pairs={{0,4},{4,0},{1,5},{5,1},{2,6},{6,2},{3,7},{7,3},{8,12},{12,8},{9,1... | collective-permute-start | bytes 1781768 | tf_op jit(solution)/shard_map/ppermute | solution.py:258
  132.0 35.9 %collective-permute-start.26 = (bf16[580,512]{1,0:T(8,128)(2,1)}, bf16[580,512]{1,0:T(8,128)(2,1)}, u32[]{:S(2)}, u32[]{:S(2)}) collective-permute-start(bf16[580,512]{1,0:T(8,128)(2,1)} %reshape.2088), channel_id=1, source_target_pairs={{0,4},{4,0},{1,5},{5,1},{2,6},{6,2},{3,7},{7,3},{8,12},{12,8},{9,1... | collective-permute-start | bytes 1781768 | tf_op jit(solution)/shard_map/ppermute | solution.py:258
  141.1 18.6 %collective-permute-start.2 = (bf16[4,32,1664]{2,1,0:T(8,128)(2,1)}, bf16[4,32,1664]{2,1,0:T(8,128)(2,1)}, u32[]{:S(2)}, u32[]{:S(2)}) collective-permute-start(bf16[4,32,1664]{2,1,0:T(8,128)(2,1)} %get-tuple-element.184), channel_id=1, source_target_pairs={{0,4},{4,0},{1,5},{5,1},{2,6},{6,2},{3,7},{7,3},{8,12},{12,8},{9,1... | collective-permute-start | bytes 1277960 | tf_op jit(solution)/shard_map/ppermute | solution.py:258
  142.7 60.2 %collective-permute-start.21 = (bf16[256,1024]{1,0:T(8,128)(2,1)}, bf16[256,1024]{1,0:T(8,128)(2,1)}, u32[]{:S(2)}, u32[]{:S(2)}) collective-permute-start(bf16[256,1024]{1,0:T(8,128)(2,1)} %bitcast.73), channel_id=1, source_target_pairs={{0,16},{16,0},{1,17},{17,1},{2,18},{18,2},{3,19},{19,3},{4,20},{20... | collective-permute-start | bytes 1572872 | tf_op jit(solution)/shard_map/ppermute | solution.py:266
  159.8 37.0 %collective-permute-start.19 = (bf16[256,1024]{1,0:T(8,128)(2,1)}, bf16[256,1024]{1,0:T(8,128)(2,1)}, u32[]{:S(2)}, u32[]{:S(2)}) collective-permute-start(bf16[256,1024]{1,0:T(8,128)(2,1)} %bitcast.65), channel_id=1, source_target_pairs={{0,8},{8,0},{1,9},{9,1},{2,10},{10,2},{3,11},{11,3},{4,12},{12,4},... | collective-permute-start | bytes 1572872 | tf_op jit(solution)/shard_map/ppermute | solution.py:262
  163.8 23.4 %collective-permute-start.5 = (bf16[128,1664]{1,0:T(8,128)(2,1)}, bf16[128,1664]{1,0:T(8,128)(2,1)}, u32[]{:S(2)}, u32[]{:S(2)}) collective-permute-start(bf16[128,1664]{1,0:T(8,128)(2,1)} %bitcast.13), channel_id=1, source_target_pairs={{0,16},{16,0},{1,17},{17,1},{2,18},{18,2},{3,19},{19,3},{4,20},{20... | collective-permute-start | bytes 1277960 | tf_op jit(solution)/shard_map/ppermute | solution.py:266
  167.9 21.7 %collective-permute-start.3 = (bf16[128,1664]{1,0:T(8,128)(2,1)}, bf16[128,1664]{1,0:T(8,128)(2,1)}, u32[]{:S(2)}, u32[]{:S(2)}) collective-permute-start(bf16[128,1664]{1,0:T(8,128)(2,1)} %bitcast.6), channel_id=1, source_target_pairs={{0,8},{8,0},{1,9},{9,1},{2,10},{10,2},{3,11},{11,3},{4,12},{12,4},... | collective-permute-start | bytes 1277960 | tf_op jit(solution)/shard_map/ppermute | solution.py:262
  187.2 63.4 %copy-start.3 = (f32[580,1024]{1,0:T(8,128)}, f32[580,1024]{1,0:T(8,128)S(1)}, u32[]{:S(2)}) copy-start(f32[580,1024]{1,0:T(8,128)S(1)} %reshape.2100) | copy-start | bytes 7127044
  187.2 8.7 %collective-permute-start.14 = (bf16[4,32,2048]{2,1,0:T(8,128)(2,1)}, bf16[4,32,2048]{2,1,0:T(8,128)(2,1)S(1)}, u32[]{:S(2)}, u32[]{:S(2)}) collective-permute-start(bf16[4,32,2048]{2,1,0:T(8,128)(2,1)} %select_n.859), channel_id=1, source_target_pairs={{0,4},{4,0},{1,5},{5,1},{2,6},{6,2},{3,7},{7,3},{8,12},{12,8},{9,1... | collective-permute-start | bytes 1572872 | tf_op jit(solution)/shard_map/ppermute | solution.py:258
  189.6 40.8 %collective-permute-start.6 = (bf16[2,128,1664]{2,1,0:T(8,128)(2,1)S(1)}, bf16[2,128,1664]{2,1,0:T(8,128)(2,1)S(1)}, u32[]{:S(2)}, u32[]{:S(2)}) collective-permute-start(bf16[2,128,1664]{2,1,0:T(8,128)(2,1)S(1)} %maximum_select_fusion.21), channel_id=1, source_target_pairs={{0,8},{8,0},{1,9},{9,1},{2,10},{10,2},{3,11},{11,3},{4,12},{12,4},... | collective-permute-start | bytes 2555912 | tf_op jit(solution)/shard_map/ppermute | solution.py:262
  195.9 35.3 %collective-permute-start.4 = (bf16[2,128,1664]{2,1,0:T(8,128)(2,1)S(1)}, bf16[2,128,1664]{2,1,0:T(8,128)(2,1)S(1)}, u32[]{:S(2)}, u32[]{:S(2)}) collective-permute-start(bf16[2,128,1664]{2,1,0:T(8,128)(2,1)S(1)} %maximum_select_fusion.19), channel_id=1, source_target_pairs={{0,16},{16,0},{1,17},{17,1},{2,18},{18,2},{3,19},{19,3},{4,20},{20... | collective-permute-start | bytes 2555912 | tf_op jit(solution)/shard_map/ppermute | solution.py:266
  196.8 24.7 %collective-permute-start.15 = (bf16[128,2048]{1,0:T(8,128)(2,1)S(1)}, bf16[128,2048]{1,0:T(8,128)(2,1)S(1)}, u32[]{:S(2)}, u32[]{:S(2)}) collective-permute-start(bf16[128,2048]{1,0:T(8,128)(2,1)S(1)} %bitcast.429), channel_id=1, source_target_pairs={{0,8},{8,0},{1,9},{9,1},{2,10},{10,2},{3,11},{11,3},{4,12},{12,4},... | collective-permute-start | bytes 1572872 | tf_op jit(solution)/shard_map/ppermute | solution.py:262
  202.9 24.7 %collective-permute-start.17 = (bf16[128,2048]{1,0:T(8,128)(2,1)S(1)}, bf16[128,2048]{1,0:T(8,128)(2,1)S(1)}, u32[]{:S(2)}, u32[]{:S(2)}) collective-permute-start(bf16[128,2048]{1,0:T(8,128)(2,1)S(1)} %bitcast.426), channel_id=1, source_target_pairs={{0,16},{16,0},{1,17},{17,1},{2,18},{18,2},{3,19},{19,3},{4,20},{20... | collective-permute-start | bytes 1572872 | tf_op jit(solution)/shard_map/ppermute | solution.py:266
  221.6 51.8 %collective-permute-start.22 = (bf16[2,256,1024]{2,1,0:T(8,128)(2,1)}, bf16[2,256,1024]{2,1,0:T(8,128)(2,1)}, u32[]{:S(2)}, u32[]{:S(2)}) collective-permute-start(bf16[2,256,1024]{2,1,0:T(8,128)(2,1)} %maximum_select_fusion.16), channel_id=1, source_target_pairs={{0,8},{8,0},{1,9},{9,1},{2,10},{10,2},{3,11},{11,3},{4,12},{12,4},... | collective-permute-start | bytes 3145736 | tf_op jit(solution)/shard_map/ppermute | solution.py:262
  227.6 47.8 %collective-permute-start.20 = (bf16[2,256,1024]{2,1,0:T(8,128)(2,1)}, bf16[2,256,1024]{2,1,0:T(8,128)(2,1)}, u32[]{:S(2)}, u32[]{:S(2)}) collective-permute-start(bf16[2,256,1024]{2,1,0:T(8,128)(2,1)} %maximum_select_fusion.14), channel_id=1, source_target_pairs={{0,16},{16,0},{1,17},{17,1},{2,18},{18,2},{3,19},{19,3},{4,20},{20... | collective-permute-start | bytes 3145736 | tf_op jit(solution)/shard_map/ppermute | solution.py:266
  230.4 60.5 %collective-permute-start.18 = (bf16[2,128,2048]{2,1,0:T(8,128)(2,1)}, bf16[2,128,2048]{2,1,0:T(8,128)(2,1)}, u32[]{:S(2)}, u32[]{:S(2)}) collective-permute-start(bf16[2,128,2048]{2,1,0:T(8,128)(2,1)} %maximum_select_fusion.12), channel_id=1, source_target_pairs={{0,8},{8,0},{1,9},{9,1},{2,10},{10,2},{3,11},{11,3},{4,12},{12,4},... | collective-permute-start | bytes 3145736 | tf_op jit(solution)/shard_map/ppermute | solution.py:262
  231.3 62.3 %collective-permute-start.16 = (bf16[2,128,2048]{2,1,0:T(8,128)(2,1)}, bf16[2,128,2048]{2,1,0:T(8,128)(2,1)}, u32[]{:S(2)}, u32[]{:S(2)}) collective-permute-start(bf16[2,128,2048]{2,1,0:T(8,128)(2,1)} %maximum_select_fusion.10), channel_id=1, source_target_pairs={{0,16},{16,0},{1,17},{17,1},{2,18},{18,2},{3,19},{19,3},{4,20},{20... | collective-permute-start | bytes 3145736 | tf_op jit(solution)/shard_map/ppermute | solution.py:266
  273.4 13.3 %collective-permute-start.12 = (bf16[580,512]{1,0:T(8,128)(2,1)S(1)}, bf16[580,512]{1,0:T(8,128)(2,1)}, u32[]{:S(2)}, u32[]{:S(2)}) collective-permute-start(bf16[580,512]{1,0:T(8,128)(2,1)S(1)} %copy.369), channel_id=1, source_target_pairs={{0,4},{4,0},{1,5},{5,1},{2,6},{6,2},{3,7},{7,3},{8,12},{12,8},{9,1... | collective-permute-start | bytes 1781768 | tf_op jit(solution)/shard_map/ppermute | solution.py:258
  332.3 172.3 %collective-permute-start.23 = (f32[580,512]{1,0:T(8,128)}, f32[580,512]{1,0:T(8,128)}, u32[]{:S(2)}, u32[]{:S(2)}) collective-permute-start(f32[580,512]{1,0:T(8,128)} %bitcast.214), channel_id=1, source_target_pairs={{0,4},{4,0},{1,5},{5,1},{2,6},{6,2},{3,7},{7,3},{8,12},{12,8},{9,1... | collective-permute-start | bytes 3563528 | tf_op jit(solution)/shard_map/ppermute | solution.py:258
  332.7 81.9 %collective-permute-start.27 = (f32[580,1024]{1,0:T(8,128)}, f32[580,1024]{1,0:T(8,128)}, u32[]{:S(2)}, u32[]{:S(2)}) collective-permute-start(f32[580,1024]{1,0:T(8,128)} %fusion.104), channel_id=1, source_target_pairs={{0,4},{4,0},{1,5},{5,1},{2,6},{6,2},{3,7},{7,3},{8,12},{12,8},{9,1... | collective-permute-start | bytes 7127048 | tf_op jit(solution)/shard_map/ppermute | solution.py:258
  337.0 26.1 %collective-permute-start.41 = (bf16[2,128,2048]{2,1,0:T(8,128)(2,1)S(1)}, bf16[2,128,2048]{2,1,0:T(8,128)(2,1)S(1)}, u32[]{:S(2)}, u32[]{:S(2)}) collective-permute-start(bf16[2,128,2048]{2,1,0:T(8,128)(2,1)S(1)} %fusion.36), channel_id=1, source_target_pairs={{0,8},{8,0},{1,9},{9,1},{2,10},{10,2},{3,11},{11,3},{4,12},{12,4},... | collective-permute-start | bytes 3145736 | tf_op jit(solution)/shard_map/ppermute | solution.py:262
  339.7 26.6 %collective-permute-start.39 = (bf16[2,128,2048]{2,1,0:T(8,128)(2,1)}, bf16[2,128,2048]{2,1,0:T(8,128)(2,1)}, u32[]{:S(2)}, u32[]{:S(2)}) collective-permute-start(bf16[2,128,2048]{2,1,0:T(8,128)(2,1)} %fusion.35), channel_id=1, source_target_pairs={{0,16},{16,0},{1,17},{17,1},{2,18},{18,2},{3,19},{19,3},{4,20},{20... | collective-permute-start | bytes 3145736 | tf_op jit(solution)/shard_map/ppermute | solution.py:266
  350.8 34.3 %collective-permute-start.46 = (bf16[2,256,1024]{2,1,0:T(8,128)(2,1)S(1)}, bf16[2,256,1024]{2,1,0:T(8,128)(2,1)S(1)}, u32[]{:S(2)}, u32[]{:S(2)}) collective-permute-start(bf16[2,256,1024]{2,1,0:T(8,128)(2,1)S(1)} %fusion.34), channel_id=1, source_target_pairs={{0,8},{8,0},{1,9},{9,1},{2,10},{10,2},{3,11},{11,3},{4,12},{12,4},... | collective-permute-start | bytes 3145736 | tf_op jit(solution)/shard_map/ppermute | solution.py:262
  364.1 26.0 %collective-permute-start.44 = (bf16[2,256,1024]{2,1,0:T(8,128)(2,1)S(1)}, bf16[2,256,1024]{2,1,0:T(8,128)(2,1)S(1)}, u32[]{:S(2)}, u32[]{:S(2)}) collective-permute-start(bf16[2,256,1024]{2,1,0:T(8,128)(2,1)S(1)} %fusion.37), channel_id=1, source_target_pairs={{0,16},{16,0},{1,17},{17,1},{2,18},{18,2},{3,19},{19,3},{4,20},{20... | collective-permute-start | bytes 3145736 | tf_op jit(solution)/shard_map/ppermute | solution.py:266
  366.3 35.1 %collective-permute-start.42 = (bf16[128,2048]{1,0:T(8,128)(2,1)S(1)}, bf16[128,2048]{1,0:T(8,128)(2,1)S(1)}, u32[]{:S(2)}, u32[]{:S(2)}) collective-permute-start(bf16[128,2048]{1,0:T(8,128)(2,1)S(1)} %fusion.57), channel_id=1, source_target_pairs={{0,16},{16,0},{1,17},{17,1},{2,18},{18,2},{3,19},{19,3},{4,20},{20... | collective-permute-start | bytes 1572872 | tf_op jit(solution)/shard_map/ppermute | solution.py:266
  385.0 18.0 %collective-permute-start.40 = (bf16[128,2048]{1,0:T(8,128)(2,1)S(1)}, bf16[128,2048]{1,0:T(8,128)(2,1)S(1)}, u32[]{:S(2)}, u32[]{:S(2)}) collective-permute-start(bf16[128,2048]{1,0:T(8,128)(2,1)S(1)} %fusion.56), channel_id=1, source_target_pairs={{0,8},{8,0},{1,9},{9,1},{2,10},{10,2},{3,11},{11,3},{4,12},{12,4},... | collective-permute-start | bytes 1572872 | tf_op jit(solution)/shard_map/ppermute | solution.py:262
  390.1 20.7 %collective-permute-start.47 = (bf16[256,1024]{1,0:T(8,128)(2,1)}, bf16[256,1024]{1,0:T(8,128)(2,1)}, u32[]{:S(2)}, u32[]{:S(2)}) collective-permute-start(bf16[256,1024]{1,0:T(8,128)(2,1)} %fusion.59), channel_id=1, source_target_pairs={{0,16},{16,0},{1,17},{17,1},{2,18},{18,2},{3,19},{19,3},{4,20},{20... | collective-permute-start | bytes 1572872 | tf_op jit(solution)/shard_map/ppermute | solution.py:266
  401.3 11.0 %collective-permute-start.45 = (bf16[256,1024]{1,0:T(8,128)(2,1)}, bf16[256,1024]{1,0:T(8,128)(2,1)}, u32[]{:S(2)}, u32[]{:S(2)}) collective-permute-start(bf16[256,1024]{1,0:T(8,128)(2,1)} %fusion.58), channel_id=1, source_target_pairs={{0,8},{8,0},{1,9},{9,1},{2,10},{10,2},{3,11},{11,3},{4,12},{12,4},... | collective-permute-start | bytes 1572872 | tf_op jit(solution)/shard_map/ppermute | solution.py:262
  404.3 125.9 %all-to-all-start.10 = ((bf16[4,2,32,2048]{3,2,1,0:T(8,128)(2,1)}), bf16[4,2,32,2048]{3,2,1,0:T(8,128)(2,1)}, u32[]{:S(2)}, u32[]{:S(2)}) async-start(bf16[4,2,32,2048]{3,2,1,0:T(8,128)(2,1)} %copy.418), calls=%async_computation.10 | async-start | bytes 2097152 | tf_op jit(solution)/shard_map/all_to_all | solution.py:270
  472.0 46.3 %collective-permute-start.37 = (bf16[2,64,1024]{2,1,0:T(8,128)(2,1)}, bf16[2,64,1024]{2,1,0:T(8,128)(2,1)}, u32[]{:S(2)}, u32[]{:S(2)}) collective-permute-start(bf16[2,64,1024]{2,1,0:T(8,128)(2,1)} %fusion.63), channel_id=1, source_target_pairs={{0,8},{8,0},{1,9},{9,1},{2,10},{10,2},{3,11},{11,3},{4,12},{12,4},... | collective-permute-start | bytes 786440 | tf_op jit(solution)/shard_map/ppermute | solution.py:262
  473.5 47.5 %collective-permute-start.35 = (bf16[2,64,1024]{2,1,0:T(8,128)(2,1)}, bf16[2,64,1024]{2,1,0:T(8,128)(2,1)}, u32[]{:S(2)}, u32[]{:S(2)}) collective-permute-start(bf16[2,64,1024]{2,1,0:T(8,128)(2,1)} %fusion.64), channel_id=1, source_target_pairs={{0,16},{16,0},{1,17},{17,1},{2,18},{18,2},{3,19},{19,3},{4,20},{20... | collective-permute-start | bytes 786440 | tf_op jit(solution)/shard_map/ppermute | solution.py:266
  498.2 29.6 %collective-permute-start.28 = (f32[580,640]{1,0:T(8,128)}, f32[580,640]{1,0:T(8,128)}, u32[]{:S(2)}, u32[]{:S(2)}) collective-permute-start(f32[580,640]{1,0:T(8,128)} %select_maximum_fusion), channel_id=1, source_target_pairs={{0,4},{4,0},{1,5},{5,1},{2,6},{6,2},{3,7},{7,3},{8,12},{12,8},{9,1... | collective-permute-start | bytes 4454408 | tf_op jit(solution)/shard_map/ppermute | solution.py:258
  519.4 6.0 collective-permute-start.38
  522.0 5.7 collective-permute-start.36
  530.2 29.9 %all-to-all-start.11 = ((bf16[4,128,1024]{2,1,0:T(8,128)(2,1)}), bf16[4,128,1024]{2,1,0:T(8,128)(2,1)}, u32[]{:S(2)}, u32[]{:S(2)}) async-start(bf16[4,128,1024]{2,1,0:T(8,128)(2,1)} %bitcast.163), calls=%async_computation.11 | async-start | bytes 2097152 | tf_op jit(solution)/shard_map/all_to_all | solution.py:270
  543.5 20.6 %collective-permute-start.32 = (bf16[2,128,1664]{2,1,0:T(8,128)(2,1)S(1)}, bf16[2,128,1664]{2,1,0:T(8,128)(2,1)}, u32[]{:S(2)}, u32[]{:S(2)}) collective-permute-start(bf16[2,128,1664]{2,1,0:T(8,128)(2,1)S(1)} %fusion.47), channel_id=1, source_target_pairs={{0,8},{8,0},{1,9},{9,1},{2,10},{10,2},{3,11},{11,3},{4,12},{12,4},... | collective-permute-start | bytes 2555912 | tf_op jit(solution)/shard_map/ppermute | solution.py:262
  548.0 31.2 %collective-permute-start.30 = (bf16[2,128,1664]{2,1,0:T(8,128)(2,1)}, bf16[2,128,1664]{2,1,0:T(8,128)(2,1)}, u32[]{:S(2)}, u32[]{:S(2)}) collective-permute-start(bf16[2,128,1664]{2,1,0:T(8,128)(2,1)} %fusion.46), channel_id=1, source_target_pairs={{0,16},{16,0},{1,17},{17,1},{2,18},{18,2},{3,19},{19,3},{4,20},{20... | collective-permute-start | bytes 2555912 | tf_op jit(solution)/shard_map/ppermute | solution.py:266
  560.0 12.5 %all-to-all-start.9 = ((bf16[4,32,1024]{2,1,0:T(8,128)(2,1)}), bf16[4,32,1024]{2,1,0:T(8,128)(2,1)}, u32[]{:S(2)}, u32[]{:S(2)}) async-start(bf16[4,32,1024]{2,1,0:T(8,128)(2,1)} %bitcast.139), calls=%async_computation.9 | async-start | bytes 524288 | tf_op jit(solution)/shard_map/all_to_all | solution.py:270
  572.6 18.7 %all-to-all-start.5 = ((bf16[4,145,512]{2,1,0:T(8,128)(2,1)}), bf16[4,145,512]{2,1,0:T(8,128)(2,1)}, u32[]{:S(2)}, u32[]{:S(2)}) async-start(bf16[4,145,512]{2,1,0:T(8,128)(2,1)} %reshape.2085), calls=%async_computation.5 | async-start | bytes 1245184 | tf_op jit(solution)/shard_map/all_to_all | solution.py:270
  578.7 16.1 %collective-permute-start.33 = (bf16[128,1664]{1,0:T(8,128)(2,1)}, bf16[128,1664]{1,0:T(8,128)(2,1)}, u32[]{:S(2)}, u32[]{:S(2)}) collective-permute-start(bf16[128,1664]{1,0:T(8,128)(2,1)} %fusion.62), channel_id=1, source_target_pairs={{0,16},{16,0},{1,17},{17,1},{2,18},{18,2},{3,19},{19,3},{4,20},{20... | collective-permute-start | bytes 1277960 | tf_op jit(solution)/shard_map/ppermute | solution.py:266
  581.8 14.4 %collective-permute-start.31 = (bf16[128,1664]{1,0:T(8,128)(2,1)S(1)}, bf16[128,1664]{1,0:T(8,128)(2,1)S(1)}, u32[]{:S(2)}, u32[]{:S(2)}) collective-permute-start(bf16[128,1664]{1,0:T(8,128)(2,1)S(1)} %fusion.61), channel_id=1, source_target_pairs={{0,8},{8,0},{1,9},{9,1},{2,10},{10,2},{3,11},{11,3},{4,12},{12,4},... | collective-permute-start | bytes 1277960 | tf_op jit(solution)/shard_map/ppermute | solution.py:262
  591.3 18.4 %all-to-all-start.7 = ((bf16[4,145,512]{2,1,0:T(8,128)(2,1)}), bf16[4,145,512]{2,1,0:T(8,128)(2,1)S(1)}, u32[]{:S(2)}, u32[]{:S(2)}) async-start(bf16[4,145,512]{2,1,0:T(8,128)(2,1)} %reshape.2092), calls=%async_computation.7 | async-start | bytes 1245184 | tf_op jit(solution)/shard_map/all_to_all | solution.py:270
  609.7 24.4 %all-to-all-start.8 = ((bf16[4,2,32,1664]{3,2,1,0:T(8,128)(2,1)}), bf16[4,2,32,1664]{3,2,1,0:T(8,128)(2,1)S(1)}, u32[]{:S(2)}, u32[]{:S(2)}) async-start(bf16[4,2,32,1664]{3,2,1,0:T(8,128)(2,1)} %bitcast.385), calls=%async_computation.8 | async-start | bytes 1703936 | tf_op jit(solution)/shard_map/all_to_all | solution.py:270
  613.5 6.1 collective-permute-start.43
  614.7 8.2 %collective-permute-start.24 = (bf16[2,145,512]{2,1,0:T(8,128)(2,1)S(1)}, bf16[2,145,512]{2,1,0:T(8,128)(2,1)S(1)}, u32[]{:S(2)}, u32[]{:S(2)}) collective-permute-start(bf16[2,145,512]{2,1,0:T(8,128)(2,1)S(1)} %get-tuple-element.170), channel_id=1, source_target_pairs={{0,4},{4,0},{1,5},{5,1},{2,6},{6,2},{3,7},{7,3},{8,12},{12,8},{9,1... | collective-permute-start | bytes 890888 | tf_op jit(solution)/shard_map/ppermute | solution.py:258
  623.1 3.2 collective-permute-start.29
  635.0 1.5 collective-permute-start.34
  (87 other events, 560.8 us)

commit v2 on v1

--- a/solution.py
+++ b/solution.py
@@ -276,8 +276,38 @@
     )
 
 
-def take(index, value, axis):
-    return lax.dynamic_index_in_dim(value, index, axis, keepdims=False)
+def side_by_side(index, mine, other):
+    return jnp.where(
+        index == 0,
+        jnp.concatenate([mine, other], axis=-1),
+        jnp.concatenate([other, mine], axis=-1),
+    )
+
+
+def half_cols(index, value):
+    middle = value.shape[-1] // 2
+    return jnp.where(index == 0, value[..., :middle], value[..., middle:])
+
+
+def take(index, value):
+    return lax.dynamic_index_in_dim(value, index, 0, keepdims=False)
+
+
+def after(value, *earlier):
+    return lax.optimization_barrier((value,) + earlier)[0]
+
+
+def parity_cols(value, size):
+    count = value.shape[-1] // size
+    parts = [value[..., k * size : (k + 1) * size] for k in range(count)]
+    return parts[0::2] + parts[1::2]
+
+
+def natural_cols(even, odd, size):
+    parts = []
+    for k in range(even.shape[-1] // size):
+        parts += [even[..., k * size : (k + 1) * size], odd[..., k * size : (k + 1) * size]]
+    return jnp.concatenate(parts, axis=-1)
 
 
 def gather_z(shard):
@@ -300,25 +330,27 @@
     return jnp.stack([first_all, second_all], axis=2).reshape(4 * rows.shape[0], rows.shape[1])
 
 
-def scatter_plane(total):
+def scatter_plane(left, right):
+    low = jnp.bfloat16
     here_x, here_y = (lax.axis_index("x"), lax.axis_index("y"))
-    rows = total.shape[0] // 4
-    half = rows // 2
-    blocks = total.reshape(2, 2, 2, half, total.shape[1])
-    first, second = (blocks[:, :, 0], blocks[:, :, 1])
-    first_got = swap_y(take(1 - here_y, first, 0).astype(jnp.bfloat16))
-    second_got = swap_x(take(1 - here_x, second, 1).astype(jnp.bfloat16))
-    first_sum = take(here_y, first, 0) + first_got
-    second_sum = take(here_x, second, 1) + second_got
-    first_last = swap_x(take(1 - here_x, first_sum, 0).astype(jnp.bfloat16))
-    second_last = swap_y(take(1 - here_y, second_sum, 0).astype(jnp.bfloat16))
-    return jnp.concatenate(
-        [
-            take(here_x, first_sum, 0) + first_last,
-            take(here_y, second_sum, 0) + second_last,
-        ],
-        axis=0,
-    )
+    rows = left.shape[1] // 4
+    cols = right.shape[1] // 2
+    first, second = (right[:, :cols], right[:, cols:])
+
+    def along_x(index):
+        return jnp.concatenate(
+            [half_cols(index, left[:, : 2 * rows]), half_cols(index, left[:, 2 * rows :])], axis=1
+        )
+
+    first_got = swap_y(contract_rows(half_cols(1 - here_y, left), first).astype(low))
+    second_got = swap_x(contract_rows(along_x(1 - here_x), second).astype(low))
+    first_sum = contract_rows(half_cols(here_y, left), first) + first_got
+    second_sum = contract_rows(along_x(here_x), second) + second_got
+    first_sum = first_sum.reshape(2, rows, cols)
+    second_sum = second_sum.reshape(2, rows, cols)
+    first_last = swap_x(take(1 - here_x, first_sum).astype(low))
+    second_last = swap_y(take(1 - here_y, second_sum).astype(low))
+    return (take(here_x, first_sum) + first_last, take(here_y, second_sum) + second_last)
 
 
 def scatter_z(parts):
@@ -349,92 +381,105 @@
     low = jnp.bfloat16
     slot_count, tok_dev, width = tokens_in.shape
     core, place = (lax.axis_index("core"), lax.axis_index("z"))
+    here_x, here_y = (lax.axis_index("x"), lax.axis_index("y"))
     depth = lax.axis_size("z")
-    planes = lax.axis_size("y") * lax.axis_size("x")
+    planes = 4
     length = depth * tok_dev
     block = width // (2 * planes)
     part_rows = w_query.shape[0]
     half = width // 2
-    ff_width = w_up.shape[1]
-    ff_half = ff_width // 2
-    ff_block = ff_width // (2 * planes)
+    ff_half = w_up.shape[1] // 2
+    ff_block = ff_half // planes
     ff_rows = w_down.shape[0]
-
-    def split_cols(value, size):
-        lead = value.shape[:-1]
-        view = value.reshape(lead + (-1, 2, size))
-        even, odd = (view[..., 0, :], view[..., 1, :])
-        mine = jnp.where(core == 0, even, odd)
-        other = jnp.where(core == 0, odd, even)
-        return (mine.reshape(lead + (-1,)), other.reshape(lead + (-1,)))
-
-    def join_cols(mine, other, size):
-        lead = mine.shape[:-1]
-        view = lead + (-1, size)
-        return in_order(core, mine.reshape(view), other.reshape(view), len(lead) + 1).reshape(
-            lead + (-1,)
-        )
-
-    def to_image(local):
-        mine, other = split_cols(local, block)
-        images = in_order(core, mine, swap_core(other), 0)
-        images = images.reshape(2 * slot_count, tok_dev, half)
-        mine = trade_z(images).reshape(length, half)
-        return join_cols(mine, swap_core(mine), block)
+    count = 8
+    small_size = count * part_rows + b_up.shape[0]
+
+    def to_image(local, *earlier):
+        images = in_order(
+            core, half_cols(core, local), swap_core(half_cols(1 - core, local)), 0
+        ).reshape(2 * slot_count, tok_dev, half)
+        mine = trade_z(after(images, *earlier)).reshape(length, half)
+        return (side_by_side(core, mine, swap_core(mine)), mine)
 
     def to_tokens(mine):
         images = trade_z(mine.reshape(depth, tok_dev, half))
         images = images.reshape(2, slot_count, tok_dev, half)
-        other = swap_core(take(1 - core, images, 0))
-        return join_cols(take(core, images, 0), other, block)
-
-    vectors = (ln1_gain, ln1_shift, b_query, b_value, b_out, ln2_gain, ln2_shift, b_down)
-    small = jnp.concatenate([vector.astype(low) for vector in vectors] + [b_up.astype(low)])
-    small_rows = jnp.pad(small, (0, part_rows * 128 - small.shape[0])).reshape(part_rows, 128)
-
+        return side_by_side(core, take(core, images), swap_core(take(1 - core, images)))
+
+    vectors = (ln1_gain, ln1_shift, b_query, b_value, b_out, ln2_gain, ln2_shift, b_down, b_up)
+    small = jnp.concatenate([vector.astype(low) for vector in vectors])
+    small_rows = jnp.pad(small, (0, part_rows * 128 - small_size)).reshape(part_rows, 128)
+    columns = [parity_cols(w, block) for w in (w_query, w_key, w_value)]
+    evens = [part for parts in columns for part in parts[:planes]]
+    odds = [part for parts in columns for part in parts[planes:]]
     project = gather_z(
-        jnp.concatenate(
-            [w_query.astype(low), w_key.astype(low), w_value.astype(low), small_rows], axis=1
-        )
-    )
-    image_in = to_image(tokens_in)
-    mine, other = split_cols(project[..., : 3 * width], block)
-    small_part = project[..., 3 * width :]
+        jnp.concatenate([part.astype(low) for part in evens + odds] + [small_rows], axis=1)
+    )
+
+    up_local = jnp.concatenate([part.astype(low) for part in parity_cols(w_up, ff_block)], axis=1)
+    up_pair = in_order(core, half_cols(core, up_local), swap_core(half_cols(1 - core, up_local)), 0)
+    up_pair = up_pair.reshape(2 * part_rows, ff_half)
+    shard = jnp.concatenate(
+        [w_down.astype(low), up_pair[:, :width], up_pair[:, width:], w_out.astype(low)], axis=0
+    )
+    gathered = lax.all_gather(shard, ("y", "x", "z"), axis=0, tiled=False)
+
+    image_in, token_half = to_image(tokens_in, project)
+    small_part = project[..., 6 * half :]
     project_pair = in_order(
         core,
-        jnp.concatenate([mine, small_part], axis=-1),
-        swap_core(jnp.concatenate([other, small_part], axis=-1)),
+        jnp.concatenate([half_cols(core, project[..., : 6 * half]), small_part], axis=-1),
+        swap_core(
+            jnp.concatenate([half_cols(1 - core, project[..., : 6 * half]), small_part], axis=-1)
+        ),
         0,
     )
     project_all = gather_plane(project_pair.reshape(2 * depth * part_rows, 3 * half + 128))
     qkv_w = project_all[:, : 3 * half]
-    small_all = project_all[:, 3 * half :].reshape(-1, part_rows * 128)[:, : small.shape[0]]
+    small_all = project_all[:, 3 * half :].reshape(-1, part_rows * 128)[:, :small_size]
     small_all = small_all.astype(jnp.float32)
-    count = len(vectors)
     wide = small_all[:, : count * part_rows].reshape(-1, count, part_rows)
     wide = wide.transpose(1, 0, 2).reshape(count, width)
     gain_one, shift_one, query_b, value_b, out_b, gain_two, shift_two, down_b = [
         wide[index] for index in range(count)
     ]
-    query_b = split_cols(query_b, block)[0]
-    value_b = split_cols(value_b, block)[0]
-    up_b = split_cols(small_all[:, count * part_rows :].reshape(ff_width), ff_block)[0]
-
-    out_mine = gather_plane(gather_z(w_out.astype(low)).reshape(depth * part_rows, width))
+
+    def own_cols(vector, size):
+        return jnp.where(
+            core == 0,
+            jnp.concatenate(parity_cols(vector, size)[:planes]),
+            jnp.concatenate(parity_cols(vector, size)[planes:]),
+        )
+
+    query_b = own_cols(query_b, block)
+    value_b = own_cols(value_b, block)
+    up_b = own_cols(small_all[:, count * part_rows :].reshape(2 * ff_half), ff_block)
+
+    down_w = gathered[:, :ff_rows].reshape(ff_half, width)
+
+    def by_feature(rows):
+        return (
+            rows.reshape(planes, depth, 2, part_rows, width)
+            .transpose(0, 2, 1, 3, 4)
+            .reshape(width, width)
+        )
+
+    up_w = jnp.concatenate(
+        [
+            by_feature(gathered[:, ff_rows : ff_rows + 2 * part_rows]),
+            by_feature(gathered[:, ff_rows + 2 * part_rows : ff_rows + 4 * part_rows]),
+        ],
+        axis=1,
+    )
+    out_mine = gathered[:, ff_rows + 4 * part_rows :].reshape(half, width)
     out_other = swap_core(out_mine)
-
-    up_part = gather_z(w_up.astype(low))
-    mine, other = split_cols(up_part, ff_block)
-    up_pair = in_order(core, mine, swap_core(other), 0)
-    up_w = gather_plane(up_pair.reshape(2 * depth * part_rows, ff_half))
-    down_w = gather_plane(gather_z(w_down.astype(low)).reshape(depth * ff_rows, width))
 
     live_slot = jnp.arange(slot_count) < group_count[0]
     live_low = live_slot.astype(low)[:, None, None]
-    upstream_low = to_image(cotangent * live_low)
+    upstream_low, upstream_half = to_image(cotangent * live_low, image_in)
 
     owner, slot = (place // slot_count, place % slot_count)
-    mask_mine = take(slot, key_mask, 0).astype(jnp.float32)[None, :]
+    mask_mine = take(slot, key_mask).astype(jnp.float32)[None, :]
     key_keep = jnp.where(core == owner, mask_mine, swap_core(mask_mine))[0]
 
     inputs = image_in.astype(jnp.float32)
@@ -450,16 +495,17 @@
     hidden = product(normed_two, up_w) + up_b
     gate_sig = jax.nn.sigmoid(SLOPE * hidden)
     activated = (hidden * gate_sig).astype(low)
-    grad_down = contract_rows(activated, upstream_low)
+    down_first, down_second = scatter_plane(activated, upstream_low)
     grad_act = contract_cols(upstream_low, down_w)
     grad_hidden = (grad_act * (gate_sig + SLOPE * hidden * gate_sig * (1.0 - gate_sig))).astype(low)
     grad_two = contract_cols(grad_hidden, up_w)
     grad_normed_two = grad_two + swap_core(grad_two)
-    grad_up = contract_rows(normed_two, grad_hidden)
+    up_first, up_second = scatter_plane(normed_two, grad_hidden)
 
     result = product(activated, down_w)
-    mine, other = split_cols(result, block)
-    result = split_cols(middle + down_b, block)[0] + (mine + swap_core(other))
+    result = half_cols(core, middle + down_b) + (
+        half_cols(core, result) + swap_core(half_cols(1 - core, result))
+    )
     block_out = to_tokens(result.astype(low)) * live_low
 
     upstream = upstream_low.astype(jnp.float32)
@@ -469,10 +515,10 @@
     grad_middle = upstream + grad_mid
     branch_low = grad_middle.astype(low)
     grad_mixed = contract_cols(branch_low, out_mine).astype(low)
-    grad_out = contract_rows(mixed, branch_low)
+    out_first, out_second = scatter_plane(mixed, branch_low)
     grad_stacked = attend_back((stacked, grad_mixed, log_total, key_keep))
     grad_qkv = grad_stacked.reshape(length, 3 * half)
-    grad_project = contract_rows(normed_one, grad_qkv)
+    project_first, project_second = scatter_plane(normed_one, grad_qkv)
 
     grad_one = contract_cols(grad_qkv, qkv_w)
     scaled = grad_one * gain_one
@@ -483,74 +529,109 @@
         ],
         axis=1,
     )
-    mine, other = split_cols(grad_one, block)
-    got = swap_core(jnp.concatenate([other, jnp.pad(sums, ((0, 0), (0, 126)))], axis=1))
-    grad_normed_one = mine + got[:, :half]
+    got = swap_core(
+        jnp.concatenate(
+            [half_cols(1 - core, grad_one), jnp.pad(sums, ((0, 0), (0, 126)))], axis=1
+        )
+    )
+    grad_normed_one = half_cols(core, grad_one) + got[:, :half]
     means = (sums + got[:, half : half + 2]) / width
-    normal_mine = split_cols(normal_one, block)[0]
+    normal_mine = half_cols(core, normal_one)
     grad_first = inverse_one * (
-        grad_normed_one * split_cols(gain_one, block)[0]
-        - means[:, :1]
-        - normal_mine * means[:, 1:]
-    )
-    input_grad = to_tokens((split_cols(grad_middle, block)[0] + grad_first).astype(low))
-
-    grad_gain_one = jnp.sum(grad_normed_one * normal_mine, axis=0)
-    grad_shift_one = jnp.sum(grad_normed_one, axis=0)
+        grad_normed_one * half_cols(core, gain_one) - means[:, :1] - normal_mine * means[:, 1:]
+    )
+    input_grad = to_tokens((half_cols(core, grad_middle) + grad_first).astype(low))
+
     bias_qkv = jnp.sum(grad_qkv.astype(jnp.float32), axis=0)
-    small_grads = (
-        grad_gain_one,
-        grad_shift_one,
-        bias_qkv[:half],
-        bias_qkv[2 * half :],
-        split_cols(jnp.sum(branch_low.astype(jnp.float32), axis=0), block)[0],
-        split_cols(grad_gain_two, block)[0],
-        split_cols(grad_shift_two, block)[0],
-        split_cols(jnp.sum(upstream, axis=0), block)[0],
-    )
-    small_wide = jnp.stack(small_grads).reshape(count, planes * depth, part_rows)
-    small_wide = small_wide.transpose(1, 0, 2).reshape(planes * depth, count * part_rows)
-    grad_up_b = jnp.sum(grad_hidden.astype(jnp.float32), axis=0)
-    small_wide = jnp.concatenate([small_wide, grad_up_b.reshape(planes * depth, -1)], axis=1)
-    small_wide = jnp.pad(small_wide, ((0, 0), (0, part_rows * 128 - small.shape[0])))
-    small_wide = jnp.broadcast_to(
-        small_wide.reshape(planes, 1, depth * part_rows, 128),
-        (planes, 2, depth * part_rows, 128),
-    ).reshape(width, 128)
-
-    down_rows = scatter_z(scatter_plane(grad_down).reshape(depth, ff_rows, width))
-
-    def own_rows(total, cols, size):
-        by_z = scatter_plane(total).reshape(2, depth, part_rows, cols).transpose(1, 0, 2, 3)
-        pair = scatter_z(by_z)
-        mine, other = (take(core, pair, 0), swap_core(take(1 - core, pair, 0)))
-        return (mine, other)
-
-    mine, other = own_rows(grad_up, ff_half, ff_block)
-    up_rows = join_cols(mine, other, ff_block)
-    out_rows = scatter_z(scatter_plane(grad_out).reshape(depth, part_rows, width))
-    mine, other = own_rows(
-        jnp.concatenate([grad_project, small_wide], axis=1), 3 * half + 128, block
-    )
-    project_rows = join_cols(mine[:, : 3 * half], other[:, : 3 * half], block)
-    small_out = mine[:, 3 * half :].reshape(-1)[: small.shape[0]]
+
+    def placed(mine):
+        none = jnp.zeros_like(mine)
+        return side_by_side(core, mine, none)
+
+    def spread(mine):
+        none = jnp.zeros_like(mine)
+        return jnp.where(
+            core == 0, natural_cols(mine, none, block), natural_cols(none, mine, block)
+        )
+
+    first_core = (core == 0).astype(jnp.float32)
+    small_grads = jnp.stack(
+        [
+            placed(jnp.sum(grad_normed_one * normal_mine, axis=0)),
+            placed(jnp.sum(grad_normed_one, axis=0)),
+            spread(bias_qkv[:half]),
+            spread(bias_qkv[2 * half :]),
+            first_core * jnp.sum(branch_low.astype(jnp.float32), axis=0),
+            first_core * grad_gain_two,
+            first_core * grad_shift_two,
+            placed(jnp.sum(upstream_half.astype(jnp.float32), axis=0)),
+        ]
+    )
+    small_wide = small_grads.reshape(count, 2 * planes * depth, part_rows)
+    small_wide = small_wide.transpose(1, 0, 2).reshape(planes, 2, depth, count * part_rows)
+    grad_up_b = jnp.sum(grad_hidden.astype(jnp.float32), axis=0).reshape(planes, depth, -1)
+    grad_up_b = in_order(core, grad_up_b, jnp.zeros_like(grad_up_b), 1)
+    small_wide = jnp.concatenate([small_wide, grad_up_b], axis=-1).reshape(2, 2, -1)
+    small_sum = take(here_y, small_wide) + swap_y(take(1 - here_y, small_wide))
+    small_sum = take(here_x, small_sum) + swap_x(take(1 - here_x, small_sum))
+    small_sum = small_sum.reshape(2, depth, small_size).transpose(1, 0, 2)
+    small_sum = jnp.pad(small_sum, ((0, 0), (0, 0), (0, part_rows * 128 - small_size)))
+    small_sum = small_sum.reshape(depth, 2, part_rows, 128)
+
+    down_rows = scatter_z(
+        jnp.concatenate([down_first, down_second], axis=1).reshape(depth, ff_rows, width)
+    )
+
+    def by_place(rows):
+        return rows.reshape(2, depth, part_rows, -1).transpose(1, 0, 2, 3)
+
+    wide_parts = scatter_z(
+        jnp.concatenate(
+            [
+                by_place(up_first).reshape(depth, 2 * part_rows, width),
+                by_place(up_second).reshape(depth, 2 * part_rows, width),
+                jnp.concatenate([out_first, out_second], axis=1).reshape(depth, part_rows, width),
+            ],
+            axis=1,
+        )
+    )
+    out_rows = wide_parts[4 * part_rows :]
+    up_pair = jnp.concatenate(
+        [wide_parts[: 2 * part_rows], wide_parts[2 * part_rows : 4 * part_rows]], axis=1
+    ).reshape(2, part_rows, ff_half)
+    mine, other = (take(core, up_pair), swap_core(take(1 - core, up_pair)))
+    up_rows = natural_cols(
+        jnp.where(core == 0, mine, other), jnp.where(core == 0, other, mine), ff_block
+    )
+
+    project_pair = scatter_z(
+        jnp.concatenate([by_place(project_first), by_place(project_second), small_sum], axis=-1)
+    )
+    mine, other = (take(core, project_pair), swap_core(take(1 - core, project_pair)))
+    even = jnp.where(core == 0, mine, other)
+    odd = jnp.where(core == 0, other, mine)
+    query_rows, key_rows, value_rows = [
+        natural_cols(even[:, k * half : (k + 1) * half], odd[:, k * half : (k + 1) * half], block)
+        for k in range(3)
+    ]
+    small_out = (mine[:, 3 * half :] + other[:, 3 * half :]).reshape(-1)
     pieces = [small_out[k * part_rows : (k + 1) * part_rows] for k in range(count)]
     return (
         block_out,
         input_grad,
         pieces[0],
         pieces[1],
-        project_rows[:, :width],
+        query_rows,
         pieces[2],
-        project_rows[:, width : 2 * width],
-        project_rows[:, 2 * width :],
+        key_rows,
+        value_rows,
         pieces[3],
         out_rows,
         pieces[4],
         pieces[5],
         pieces[6],
         up_rows,
-        small_out[count * part_rows :],
+        small_out[count * part_rows : small_size],
         down_rows,
         pieces[7],
     )

time: 647 us -> 483 us (0.75)
  local copies, waits for them, and re-layouts: 173 us -> 52.8 us
  other arithmetic: 125 us -> 71.3 us
  starting transfers between devices: 85 us -> 63 us
  waiting for transfers between devices: 175 us -> 193 us
  between operations: 4.07 us -> 17.3 us
    ppermute x16 -> x11, waiting for transfers between devices: 18.7 us -> 60.9 us  [swap_y(): return lax.ppermute(value, 'y', [(0, 1), (1, 0)])]
    all_to_all x12 -> x8, waiting for transfers between devices: 111 us -> 89.6 us  [trade_z(): return lax.all_to_all(value, 'z', split_axis=0, concat_axis=0, tiled=True)]
    unnamed x198 -> x177, local copies, waits for them, and re-layouts: 31.3 us -> 11.8 us
    reshape x12 -> x7, local copies, waits for them, and re-layouts: 21.6 us -> 2.6 us  [the longest x2 2.25 us: to_image(): mine = trade_z(after(images, *earlier)).reshape(length, half)]
    select_n x24 -> x9, other arithmetic: 28.1 us -> 9.85 us  [in_order(): jnp.where(index == 0, jnp.stack([mine, other], axis=axis), jnp.stack([oth...]
    select_n x15 -> x20, other arithmetic: 24.1 us -> 6.66 us  [the longest x10 3.78 us: half_cols(): return jnp.where(index == 0, value[..., :middle], value[..., middle:])]
    another operation x26 -> x5, local copies, waits for them, and re-layouts: 18.3 us -> 0.82 us  [the longest x4 0.82 us: own_image(): jnp.stack([placed(jnp.sum(grad_normed_one * normal_mine, axis=0)), placed...]
    ppermute x16 -> x11, waiting for transfers between devices: 43.6 us -> 26.2 us  [swap_x(): return lax.ppermute(value, 'x', [(0, 1), (1, 0)])]
  transfers between devices with their start and end apart: 60 -> 47, of which waited for: 24 -> 17; matrix products, arithmetic and copies ran while one was open for 48% -> 37% of each run, Pallas kernels for 0% -> 0%
where the time goes in v2:
time: 483 us; the launch traced here: 477 us
  waiting for transfers between devices  193 us (40%)
  matrix products  79.7 us (17%)
  other arithmetic  71.3 us (15%)
  starting transfers between devices  63 us (13%)
  local copies, waits for them, and re-layouts  52.8 us (11%)
  between operations  17.3 us (4%)
    all_to_all x8, waiting for transfers between devices, trade_z(): return lax.all_to_all(value, 'z', split_axis=0, concat_axis=0, tiled=True)  89.6 us
    ppermute x11, waiting for transfers between devices, swap_y(): return lax.ppermute(value, 'y', [(0, 1), (1, 0)])  60.9 us
    all_to_all x8, starting transfers between devices, trade_z(): return lax.all_to_all(value, 'z', split_axis=0, concat_axis=0, tiled=True)  33.3 us
    dot_general x16, matrix products, contract_rows(): lax.dot_general(left, right, (((0,), (0,)), ((), ())), preferred_element_...  26.6 us
    ppermute x11, waiting for transfers between devices, swap_x(): return lax.ppermute(value, 'x', [(0, 1), (1, 0)])  26.2 us
    all_gather x1, waiting for transfers between devices, own_image(): gathered = lax.all_gather(shard, ('y', 'x', 'z'), axis=0, tiled=False)  16.2 us
    dot_general x4, matrix products, contract_cols(): lax.dot_general(left, right, (((1,), (1,)), ((), ())), preferred_element_...  15.3 us
    dot_general x5, matrix products, product(): return jnp.dot(left, right, preferred_element_type=jnp.float32)  14.4 us
  transfers between devices with their start and end apart: 47, of which 17 were waited for; matrix products, arithmetic and copies ran while one was open for 37% of the time, Pallas kernels for 0%

profile of v2, /device:TPU:0, one launch (start us, length us, event | category | flops | bytes accessed | tf_op | source)
XLA Modules:
  0.0 477.2 jit_solution(4449597901303470606)
XLA Ops:
  17.7 5.9 %all-to-all-start = ((bf16[4,32,3200]{2,1,0:T(8,128)(2,1)}), bf16[4,32,3200]{2,1,0:T(8,128)(2,1)S(1)}, u32[]{:S(2)}, u32[]{:S(2)}) async-start(bf16[4,32,3200]{2,1,0:T(8,128)(2,1)} %broadcast_in_dim.22), calls=%async_computation | async-start | bytes 1638400 | tf_op jit(solution)/shard_map/all_to_all | solution.py:270
  25.0 32.6 %all-to-all-done = bf16[4,32,3200]{2,1,0:T(8,128)(2,1)S(1)} async-done(((bf16[4,32,3200]{2,1,0:T(8,128)(2,1)}), bf16[4,32,3200]{2,1,0:T(8,128)(2,1)S(1)}, u32[]{:S(2)}, u32[]{:S(2)}) %all-to-all-start) | async-done | bytes 819232 | tf_op jit(solution)/shard_map/all_to_all | solution.py:270
  58.1 2.0 maximum_select_fusion.9
  60.1 3.6 all-to-all-start.1
  68.6 13.6 %collective-permute-done.5 = bf16[128,1664]{1,0:T(8,128)(2,1)S(1)} collective-permute-done((bf16[128,1664]{1,0:T(8,128)(2,1)S(1)}, bf16[128,1664]{1,0:T(8,128)(2,1)S(1)}, u32[]{:S(2)}, u32[]{:S(2)}) %collective-permute-start.5) | collective-permute-done | bytes 426016 | tf_op jit(solution)/shard_map/ppermute | solution.py:266
  84.8 10.8 %all-to-all-done.1 = bf16[4,145,512]{2,1,0:T(8,128)(2,1)S(1)} async-done(((bf16[4,145,512]{2,1,0:T(8,128)(2,1)}), bf16[4,145,512]{2,1,0:T(8,128)(2,1)S(1)}, u32[]{:S(2)}, u32[]{:S(2)}) %all-to-all-start.1) | async-done | bytes 593952 | tf_op jit(solution)/shard_map/all_to_all | solution.py:270
  101.3 4.4 all-to-all-start.3
  106.2 2.8 collective-permute-done.6
  109.0 2.2 maximum_select_fusion.1
  111.2 14.4 %collective-permute-done.4 = bf16[2,128,1664]{2,1,0:T(8,128)(2,1)} collective-permute-done((bf16[2,128,1664]{2,1,0:T(8,128)(2,1)}, bf16[2,128,1664]{2,1,0:T(8,128)(2,1)}, u32[]{:S(2)}, u32[]{:S(2)}) %collective-permute-start.4) | collective-permute-done | bytes 852000 | tf_op jit(solution)/shard_map/ppermute | solution.py:266
  125.6 1.8 maximum_select_fusion
  127.7 1.8 copy-done.20
  133.3 5.2 %add_convert_fusion = bf16[580,1536]{1,0:T(8,128)(2,1)} fusion(bf16[580,1024]{1,0:T(8,128)(2,1)S(1)} %add_convert_fusion.2, bf16[1024,1664]{1,0:T(8,128)(2,1)} %bitcast.254, f32[1536]{0:T(1024)S(1)} %pad_maximum_fusion.13), kind=kOutput, calls=%fused_computation.18 | convolution fusion | flops 1826304000 | bytes 6121472 | tf_op jit(solution)/shard_map/dot_general | solution.py:31
  138.5 2.7 copy.104
  141.4 2.7 fusion.154
  144.2 1.7 fusion
  145.9 2.7 copy-done
  148.6 2.9 fusion.15
  154.4 2.1 reshape.1244
  158.0 16.2 %all-gather.3.cloned.1.call-done = bf16[4608,1024]{1,0:T(8,128)(2,1)} async-done(((bf16[288,1024]{1,0:T(8,128)(2,1)}), bf16[4608,1024]{1,0:T(8,128)(2,1)}) %all-gather.3.cloned.1.call-update) | async-done | bytes 9437200 | tf_op jit(solution)/shard_map/all_gather | solution.py:425
  179.5 3.1 slice.1118
  182.6 2.7 fusion.146
  187.0 2.4 fusion.155
  190.4 3.3 multiply_convert_fusion.2
  193.9 2.7 fusion.157
  196.6 4.4 convert_reduce_fusion
  210.7 4.2 fusion.11
  215.5 13.7 %collective-permute-done.34 = bf16[1024,512]{1,0:T(8,128)(2,1)S(1)} collective-permute-done((bf16[1024,512]{1,0:T(8,128)(2,1)S(1)}, bf16[1024,512]{1,0:T(8,128)(2,1)S(1)}, u32[]{:S(2)}, u32[]{:S(2)}) %collective-permute-start.34) | collective-permute-done | bytes 1048608 | tf_op jit(solution)/shard_map/ppermute | solution.py:266
  233.3 17.5 %collective-permute-done.25 = bf16[512,1024]{1,0:T(8,128)(2,1)S(1)} collective-permute-done((bf16[512,1024]{1,0:T(8,128)(2,1)S(1)}, bf16[512,1024]{1,0:T(8,128)(2,1)S(1)}, u32[]{:S(2)}, u32[]{:S(2)}) %collective-permute-start.25) | collective-permute-done | bytes 1048608 | tf_op jit(solution)/shard_map/ppermute | solution.py:266
  256.8 7.7 %collective-permute-done.35 = bf16[512,512]{1,0:T(8,128)(2,1)S(1)} collective-permute-done((bf16[512,512]{1,0:T(8,128)(2,1)S(1)}, bf16[512,512]{1,0:T(8,128)(2,1)S(1)}, u32[]{:S(2)}, u32[]{:S(2)}) %collective-permute-start.35) | collective-permute-done | bytes 524320 | tf_op jit(solution)/shard_map/ppermute | solution.py:262
  267.4 4.5 all-to-all-start.7
  271.9 2.9 collective-permute-done.26
  279.2 3.7 multiply_reduce_fusion.1
  283.0 2.9 convert_reduce_fusion.4
  288.1 6.4 %fusion.2 = bf16[8,64,580]{2,1,0:T(8,128)(2,1)S(1)} fusion(bf16[580,8,64]{0,2,1:T(8,128)(2,1)S(1)} %bitcast.242, f32[8,580,580]{1,2,0:T(8,128)} %copy-done, f32[8,580]{1,0:T(8,128)S(1)} %log_add_fusion), kind=kOutput, calls=%fused_computation.8 | convolution fusion | flops 349856000 | bytes 11971200 | tf_op jit(solution)/shard_map/hqk,qhd->khd/dot_general | solution.py:86
  294.5 8.4 %multiply_reduce_fusion = (f32[8,580]{1,0:T(8,128)S(1)}, f32[8,580,580]{1,2,0:T(8,128)}) fusion(f32[8,580,580]{1,2,0:T(8,128)} %copy-done, f32[8,580]{1,0:T(8,128)S(1)} %log_add_fusion, bf16[580,8,64]{0,2,1:T(8,128)(2,1)S(1)} %bitcast.243, bf16[580,8,64]{0,2,1:T(8,128)(2,1)S(1)} %bitcast.263), kind=kOutput, calls=%fused_computation.1 | convolution fusion | flops 352542560 | bytes 22754560 | tf_op jit(solution)/shard_map/qhd,khd->hqk/dot_general | solution.py:92
  302.9 6.4 %multiply_convert_fusion = bf16[8,580,580]{1,2,0:T(8,128)(2,1)S(1)} fusion(f32[8,580,580]{1,2,0:T(8,128)} %get-tuple-element.250, f32[8,580,580]{1,2,0:T(8,128)S(1)} %bitcast.228, f32[8,580]{1,0:T(8,128)S(1)} %get-tuple-element.249, f32[8,580]{1,0:T(8,128)S(1)} %log_add_fusion), kind=kLoop, calls=%fused_computation | loop fusion | flops 10764800 | bytes 26949120 | tf_op jit(solution)/shard_map/convert_element_type | solution.py:96
  309.3 1.9 convolution_multiply_fusion
  314.3 2.4 concatenate.400
  316.7 2.4 concatenate.399
  321.1 2.3 convolution_convert_fusion.8
  323.5 3.0 convolution_convert_fusion.5
  326.5 5.9 %multiply_reduce_fusion.5 = (f32[580]{0:T(1024)S(1)}, f32[580]{0:T(1024)S(1)}, f32[580,1024]{1,0:T(8,128)S(1)}, f32[580,1024]{1,0:T(8,128)}) fusion(f32[1024]{0:T(1024)S(1)} %mul.208, f32[580]{0:T(1024)S(1)} %add_rsqrt_fusion.1, f32[580]{0:T(1024)S(1)} %broadcast_multiply_fusion.7, bf16[580,1024]{1,0:T(8,128)(2,1)S(1)} %copy-done.3, ...), kind=kOutput, calls=%fused_computation.41 | convolution fusion | flops 1828678400 | bytes 10891808 | tf_op jit(solution)/shard_map/dot_general | solution.py:41
  332.4 2.7 fusion.19
  335.1 2.1 reshape.1242
  338.7 2.2 convolution_convert_fusion.7
  344.4 3.4 convolution_convert_fusion.4
  356.1 12.2 %collective-permute-done.30 = bf16[128,512]{1,0:T(8,128)(2,1)S(1)} collective-permute-done((bf16[128,512]{1,0:T(8,128)(2,1)S(1)}, bf16[128,512]{1,0:T(8,128)(2,1)S(1)}, u32[]{:S(2)}, u32[]{:S(2)}) %collective-permute-start.30) | collective-permute-done | bytes 131104 | tf_op jit(solution)/shard_map/ppermute | solution.py:262
  369.6 3.8 all-to-all-start.2
  373.4 2.8 convert_add_fusion.6
  377.4 2.0 convert_add_fusion.5
  381.2 2.3 convert_reduce_fusion.5
  383.5 4.3 all-to-all-done.2
  387.7 4.3 all-to-all-start.6
  393.8 1.8 fusion.60
  398.5 3.6 fusion.145
  404.9 1.7 collective-permute-done.22
  408.2 2.1 fusion.17
  411.4 10.3 %all-to-all-done.6 = bf16[4,160,1024]{2,1,0:T(8,128)(2,1)} async-done(((bf16[4,160,1024]{2,1,0:T(8,128)(2,1)}), bf16[4,160,1024]{2,1,0:T(8,128)(2,1)}, u32[]{:S(2)}, u32[]{:S(2)}) %all-to-all-start.6) | async-done | bytes 1310752 | tf_op jit(solution)/shard_map/all_to_all | solution.py:270
  421.8 3.5 all-to-all-start.4
  425.2 1.7 convert_reduce_fusion.3
  429.5 11.9 %all-to-all-done.4 = bf16[4,145,512]{2,1,0:T(8,128)(2,1)S(1)} async-done(((bf16[4,145,512]{2,1,0:T(8,128)(2,1)}), bf16[4,145,512]{2,1,0:T(8,128)(2,1)S(1)}, u32[]{:S(2)}, u32[]{:S(2)}) %all-to-all-start.4) | async-done | bytes 593952 | tf_op jit(solution)/shard_map/all_to_all | solution.py:270
  441.4 3.5 all-to-all-start.5
  446.1 19.8 %all-to-all-done.5 = bf16[4,2,32,1664]{3,2,1,0:T(8,128)(2,1)S(1)} async-done(((bf16[4,2,32,1664]{3,2,1,0:T(8,128)(2,1)}), bf16[4,2,32,1664]{3,2,1,0:T(8,128)(2,1)S(1)}, u32[]{:S(2)}, u32[]{:S(2)}) %all-to-all-start.5) | async-done | bytes 852000 | tf_op jit(solution)/shard_map/all_to_all | solution.py:270
  (449 shorter events, 111.2 us)
Async XLA Ops:
  7.2 8.0 %copy-start.41 = (f32[128,1024]{1,0:T(8,128)S(1)}, f32[128,1024]{1,0:T(8,128)}, u32[]{:S(2)}) copy-start(f32[128,1024]{1,0:T(8,128)} %param.36) | copy-start | bytes 1572868
  7.2 167.0 %all-gather.3.cloned.1.call-start = ((), (), s32[]{:S(2)}) async-start(), calls=%async_computation.8 | async-start | bytes 10027008 | tf_op jit(solution)/shard_map/all_gather | solution.py:425
  8.6 6.8 %collective-permute-start.8 = (bf16[32,2048]{1,0:T(8,128)(2,1)S(1)}, bf16[32,2048]{1,0:T(8,128)(2,1)S(1)}, u32[]{:S(2)}, u32[]{:S(2)}) collective-permute-start(bf16[32,2048]{1,0:T(8,128)(2,1)S(1)} %maximum_select_fusion.15), channel_id=1, source_target_pairs={{0,4},{4,0},{1,5},{5,1},{2,6},{6,2},{3,7},{7,3},{8,12},{12,8},{9,1... | collective-permute-start | bytes 393224 | tf_op jit(solution)/shard_map/ppermute | solution.py:258
  17.7 39.9 %all-to-all-start = ((bf16[4,32,3200]{2,1,0:T(8,128)(2,1)}), bf16[4,32,3200]{2,1,0:T(8,128)(2,1)S(1)}, u32[]{:S(2)}, u32[]{:S(2)}) async-start(bf16[4,32,3200]{2,1,0:T(8,128)(2,1)} %broadcast_in_dim.22), calls=%async_computation | async-start | bytes 1638400 | tf_op jit(solution)/shard_map/all_to_all | solution.py:270
  24.0 33.9 %copy-start.40 = (bf16[2,145,1024]{2,0,1:T(2,128)(2,1)S(1)}, bf16[2,145,1024]{2,0,1:T(2,128)(2,1)}, u32[]{:S(2)}) copy-start(bf16[2,145,1024]{2,0,1:T(2,128)(2,1)} %param.20) | copy-start | bytes 1781764
  24.1 34.0 %collective-permute-start = (bf16[2,145,512]{2,1,0:T(8,128)(2,1)S(1)}, bf16[2,145,512]{2,1,0:T(8,128)(2,1)}, u32[]{:S(2)}, u32[]{:S(2)}) collective-permute-start(bf16[2,145,512]{2,1,0:T(8,128)(2,1)S(1)} %get-tuple-element.170), channel_id=1, source_target_pairs={{0,4},{4,0},{1,5},{5,1},{2,6},{6,2},{3,7},{7,3},{8,12},{12,8},{9,1... | collective-permute-start | bytes 890888 | tf_op jit(solution)/shard_map/ppermute | solution.py:258
  57.7 5.9 %collective-permute-start.2 = (bf16[4,32,1664]{2,1,0:T(8,128)(2,1)S(1)}, bf16[4,32,1664]{2,1,0:T(8,128)(2,1)S(1)}, u32[]{:S(2)}, u32[]{:S(2)}) collective-permute-start(bf16[4,32,1664]{2,1,0:T(8,128)(2,1)S(1)} %get-tuple-element.224), channel_id=1, source_target_pairs={{0,4},{4,0},{1,5},{5,1},{2,6},{6,2},{3,7},{7,3},{8,12},{12,8},{9,1... | collective-permute-start | bytes 1277960 | tf_op jit(solution)/shard_map/ppermute | solution.py:258
  60.1 35.4 %all-to-all-start.1 = ((bf16[4,145,512]{2,1,0:T(8,128)(2,1)}), bf16[4,145,512]{2,1,0:T(8,128)(2,1)S(1)}, u32[]{:S(2)}, u32[]{:S(2)}) async-start(bf16[4,145,512]{2,1,0:T(8,128)(2,1)} %bitcast.2), calls=%async_computation.1 | async-start | bytes 1245184 | tf_op jit(solution)/shard_map/all_to_all | solution.py:270
  63.9 18.3 %collective-permute-start.5 = (bf16[128,1664]{1,0:T(8,128)(2,1)S(1)}, bf16[128,1664]{1,0:T(8,128)(2,1)S(1)}, u32[]{:S(2)}, u32[]{:S(2)}) collective-permute-start(bf16[128,1664]{1,0:T(8,128)(2,1)S(1)} %bitcast.256), channel_id=1, source_target_pairs={{0,16},{16,0},{1,17},{17,1},{2,18},{18,2},{3,19},{19,3},{4,20},{20... | collective-permute-start | bytes 1277960 | tf_op jit(solution)/shard_map/ppermute | solution.py:266
  65.4 2.2 collective-permute-start.13
  65.8 1.8 collective-permute-start.7
  66.1 29.7 %collective-permute-start.3 = (bf16[128,1664]{1,0:T(8,128)(2,1)S(1)}, bf16[128,1664]{1,0:T(8,128)(2,1)S(1)}, u32[]{:S(2)}, u32[]{:S(2)}) collective-permute-start(bf16[128,1664]{1,0:T(8,128)(2,1)S(1)} %bitcast.259), channel_id=1, source_target_pairs={{0,8},{8,0},{1,9},{9,1},{2,10},{10,2},{3,11},{11,3},{4,12},{12,4},... | collective-permute-start | bytes 1277960 | tf_op jit(solution)/shard_map/ppermute | solution.py:262
  82.2 14.6 %copy-start.28 = (bf16[128,1664]{1,0:T(8,128)(2,1)}, bf16[128,1664]{1,0:T(8,128)(2,1)S(1)}, u32[]{:S(2)}) copy-start(bf16[128,1664]{1,0:T(8,128)(2,1)S(1)} %collective-permute-done.5) | copy-start | bytes 1277956
  83.3 25.7 %collective-permute-start.6 = (bf16[2,128,1664]{2,1,0:T(8,128)(2,1)}, bf16[2,128,1664]{2,1,0:T(8,128)(2,1)}, u32[]{:S(2)}, u32[]{:S(2)}) collective-permute-start(bf16[2,128,1664]{2,1,0:T(8,128)(2,1)} %maximum_select_fusion.8), channel_id=1, source_target_pairs={{0,8},{8,0},{1,9},{9,1},{2,10},{10,2},{3,11},{11,3},{4,12},{12,4},... | collective-permute-start | bytes 2555912 | tf_op jit(solution)/shard_map/ppermute | solution.py:262
  95.7 5.2 %collective-permute-start.1 = (bf16[580,512]{1,0:T(8,128)(2,1)S(1)}, bf16[580,512]{1,0:T(8,128)(2,1)S(1)}, u32[]{:S(2)}, u32[]{:S(2)}) collective-permute-start(bf16[580,512]{1,0:T(8,128)(2,1)S(1)} %reshape.1231), channel_id=1, source_target_pairs={{0,4},{4,0},{1,5},{5,1},{2,6},{6,2},{3,7},{7,3},{8,12},{12,8},{9,1... | collective-permute-start | bytes 1781768 | tf_op jit(solution)/shard_map/ppermute | solution.py:258
  96.8 28.7 %collective-permute-start.4 = (bf16[2,128,1664]{2,1,0:T(8,128)(2,1)}, bf16[2,128,1664]{2,1,0:T(8,128)(2,1)}, u32[]{:S(2)}, u32[]{:S(2)}) collective-permute-start(bf16[2,128,1664]{2,1,0:T(8,128)(2,1)} %maximum_select_fusion.6), channel_id=1, source_target_pairs={{0,16},{16,0},{1,17},{17,1},{2,18},{18,2},{3,19},{19,3},{4,20},{20... | collective-permute-start | bytes 2555912 | tf_op jit(solution)/shard_map/ppermute | solution.py:266
  101.3 30.4 %copy-start.1 = (bf16[580,1024]{1,0:T(8,128)(2,1)}, bf16[580,1024]{1,0:T(8,128)(2,1)S(1)}, u32[]{:S(2)}) copy-start(bf16[580,1024]{1,0:T(8,128)(2,1)S(1)} %get-tuple-element.131) | copy-start | bytes 3563524
  101.3 53.1 %all-to-all-start.3 = ((bf16[4,145,512]{2,1,0:T(8,128)(2,1)}), bf16[4,145,512]{2,1,0:T(8,128)(2,1)}, u32[]{:S(2)}, u32[]{:S(2)}) async-start(bf16[4,145,512]{2,1,0:T(8,128)(2,1)} %bitcast.62), calls=%async_computation.3 | async-start | bytes 1245184 | tf_op jit(solution)/shard_map/all_to_all | solution.py:270
  151.4 34.2 %copy-start.8 = (bf16[8,64,580]{2,1,0:T(8,128)(2,1)}, bf16[8,64,580]{2,1,0:T(8,128)(2,1)S(1)}, u32[]{:S(2)}) copy-start(bf16[8,64,580]{2,1,0:T(8,128)(2,1)S(1)} %fusion.15) | copy-start | bytes 1781764
  153.5 33.0 %collective-permute-start.9 = (bf16[580,512]{1,0:T(8,128)(2,1)}, bf16[580,512]{1,0:T(8,128)(2,1)}, u32[]{:S(2)}, u32[]{:S(2)}) collective-permute-start(bf16[580,512]{1,0:T(8,128)(2,1)} %copy.106), channel_id=1, source_target_pairs={{0,4},{4,0},{1,5},{5,1},{2,6},{6,2},{3,7},{7,3},{8,12},{12,8},{9,1... | collective-permute-start | bytes 1781768 | tf_op jit(solution)/shard_map/ppermute | solution.py:258
  156.4 21.4 %collective-permute-start.14 = (bf16[580,512]{1,0:T(8,128)(2,1)}, bf16[580,512]{1,0:T(8,128)(2,1)}, u32[]{:S(2)}, u32[]{:S(2)}) collective-permute-start(bf16[580,512]{1,0:T(8,128)(2,1)} %reshape.1244), channel_id=1, source_target_pairs={{0,4},{4,0},{1,5},{5,1},{2,6},{6,2},{3,7},{7,3},{8,12},{12,8},{9,1... | collective-permute-start | bytes 1781768 | tf_op jit(solution)/shard_map/ppermute | solution.py:258
  158.0 19.8 %copy-start.24 = (bf16[580,512]{1,0:T(8,128)(2,1)S(1)}, bf16[580,512]{1,0:T(8,128)(2,1)}, u32[]{:S(2)}) copy-start(bf16[580,512]{1,0:T(8,128)(2,1)} %reshape.1244) | copy-start | bytes 1781764
  175.6 10.1 %copy-start.18 = (bf16[16,32,1024]{2,1,0:T(8,128)(2,1)}, bf16[16,32,1024]{2,1,0:T(8,128)(2,1)S(1)}, u32[]{:S(2)}) copy-start(bf16[16,32,1024]{2,1,0:T(8,128)(2,1)S(1)} %slice.1101) | copy-start | bytes 3145732
  175.6 11.0 %collective-permute-start.10 = (bf16[512,1024]{1,0:T(8,128)(2,1)S(1)}, bf16[512,1024]{1,0:T(8,128)(2,1)}, u32[]{:S(2)}, u32[]{:S(2)}) collective-permute-start(bf16[512,1024]{1,0:T(8,128)(2,1)S(1)} %bitcast.250), channel_id=1, source_target_pairs={{0,4},{4,0},{1,5},{5,1},{2,6},{6,2},{3,7},{7,3},{8,12},{12,8},{9,1... | collective-permute-start | bytes 3145736 | tf_op jit(solution)/shard_map/ppermute | solution.py:258
  179.5 52.7 %copy-start.12 = (bf16[580,1024]{1,0:T(8,128)(2,1)}, bf16[580,1024]{1,0:T(8,128)(2,1)S(1)}, u32[]{:S(2)}) copy-start(bf16[580,1024]{1,0:T(8,128)(2,1)S(1)} %maximum_select_fusion.3) | copy-start | bytes 3563524
  196.5 12.8 %copy-start.5 = (f32[580,1024]{1,0:T(8,128)}, f32[580,1024]{1,0:T(8,128)S(1)}, u32[]{:S(2)}) copy-start(f32[580,1024]{1,0:T(8,128)S(1)} %fusion.157) | copy-start | bytes 7127044
  203.1 26.1 %collective-permute-start.34 = (bf16[1024,512]{1,0:T(8,128)(2,1)S(1)}, bf16[1024,512]{1,0:T(8,128)(2,1)S(1)}, u32[]{:S(2)}, u32[]{:S(2)}) collective-permute-start(bf16[1024,512]{1,0:T(8,128)(2,1)S(1)} %convolution_convert_fusion.1), channel_id=1, source_target_pairs={{0,16},{16,0},{1,17},{17,1},{2,18},{18,2},{3,19},{19,3},{4,20},{20... | collective-permute-start | bytes 3145736 | tf_op jit(solution)/shard_map/ppermute | solution.py:266
  204.7 26.1 %collective-permute-start.36 = (bf16[1024,512]{1,0:T(8,128)(2,1)S(1)}, bf16[1024,512]{1,0:T(8,128)(2,1)S(1)}, u32[]{:S(2)}, u32[]{:S(2)}) collective-permute-start(bf16[1024,512]{1,0:T(8,128)(2,1)S(1)} %convolution_convert_fusion), channel_id=1, source_target_pairs={{0,8},{8,0},{1,9},{9,1},{2,10},{10,2},{3,11},{11,3},{4,12},{12,4},... | collective-permute-start | bytes 3145736 | tf_op jit(solution)/shard_map/ppermute | solution.py:262
  206.2 44.7 %collective-permute-start.25 = (bf16[512,1024]{1,0:T(8,128)(2,1)S(1)}, bf16[512,1024]{1,0:T(8,128)(2,1)S(1)}, u32[]{:S(2)}, u32[]{:S(2)}) collective-permute-start(bf16[512,1024]{1,0:T(8,128)(2,1)S(1)} %convolution_convert_fusion.3), channel_id=1, source_target_pairs={{0,16},{16,0},{1,17},{17,1},{2,18},{18,2},{3,19},{19,3},{4,20},{20... | collective-permute-start | bytes 3145736 | tf_op jit(solution)/shard_map/ppermute | solution.py:266
  208.8 44.6 %collective-permute-start.27 = (bf16[512,1024]{1,0:T(8,128)(2,1)S(1)}, bf16[512,1024]{1,0:T(8,128)(2,1)S(1)}, u32[]{:S(2)}, u32[]{:S(2)}) collective-permute-start(bf16[512,1024]{1,0:T(8,128)(2,1)S(1)} %convolution_convert_fusion.2), channel_id=1, source_target_pairs={{0,8},{8,0},{1,9},{9,1},{2,10},{10,2},{3,11},{11,3},{4,12},{12,4},... | collective-permute-start | bytes 3145736 | tf_op jit(solution)/shard_map/ppermute | solution.py:262
  210.7 121.7 %collective-permute-start.11 = (f32[580,512]{1,0:T(8,128)}, f32[580,512]{1,0:T(8,128)}, u32[]{:S(2)}, u32[]{:S(2)}) collective-permute-start(f32[580,512]{1,0:T(8,128)} %slice_select_fusion.4), channel_id=1, source_target_pairs={{0,4},{4,0},{1,5},{5,1},{2,6},{6,2},{3,7},{7,3},{8,12},{12,8},{9,1... | collective-permute-start | bytes 3563528 | tf_op jit(solution)/shard_map/ppermute | solution.py:258
  229.2 50.1 %collective-permute-start.15 = (f32[580,1024]{1,0:T(8,128)}, f32[580,1024]{1,0:T(8,128)}, u32[]{:S(2)}, u32[]{:S(2)}) collective-permute-start(f32[580,1024]{1,0:T(8,128)} %fusion.11), channel_id=1, source_target_pairs={{0,4},{4,0},{1,5},{5,1},{2,6},{6,2},{3,7},{7,3},{8,12},{12,8},{9,1... | collective-permute-start | bytes 7127048 | tf_op jit(solution)/shard_map/ppermute | solution.py:258
  230.8 33.7 %collective-permute-start.35 = (bf16[512,512]{1,0:T(8,128)(2,1)S(1)}, bf16[512,512]{1,0:T(8,128)(2,1)S(1)}, u32[]{:S(2)}, u32[]{:S(2)}) collective-permute-start(bf16[512,512]{1,0:T(8,128)(2,1)S(1)} %fusion.109), channel_id=1, source_target_pairs={{0,8},{8,0},{1,9},{9,1},{2,10},{10,2},{3,11},{11,3},{4,12},{12,4},... | collective-permute-start | bytes 1572872 | tf_op jit(solution)/shard_map/ppermute | solution.py:262
  250.9 15.3 %collective-permute-start.37 = (bf16[512,512]{1,0:T(8,128)(2,1)S(1)}, bf16[512,512]{1,0:T(8,128)(2,1)S(1)}, u32[]{:S(2)}, u32[]{:S(2)}) collective-permute-start(bf16[512,512]{1,0:T(8,128)(2,1)S(1)} %fusion.110), channel_id=1, source_target_pairs={{0,16},{16,0},{1,17},{17,1},{2,18},{18,2},{3,19},{19,3},{4,20},{20... | collective-permute-start | bytes 1572872 | tf_op jit(solution)/shard_map/ppermute | solution.py:266
  253.4 21.4 %collective-permute-start.26 = (bf16[256,1024]{1,0:T(8,128)(2,1)}, bf16[256,1024]{1,0:T(8,128)(2,1)}, u32[]{:S(2)}, u32[]{:S(2)}) collective-permute-start(bf16[256,1024]{1,0:T(8,128)(2,1)} %fusion.107), channel_id=1, source_target_pairs={{0,8},{8,0},{1,9},{9,1},{2,10},{10,2},{3,11},{11,3},{4,12},{12,4},... | collective-permute-start | bytes 1572872 | tf_op jit(solution)/shard_map/ppermute | solution.py:262
  255.8 10.5 %copy-start.34 = (f32[512,1024]{1,0:T(8,128)}, f32[512,1024]{1,0:T(8,128)S(1)}, u32[]{:S(2)}) copy-start(f32[512,1024]{1,0:T(8,128)S(1)} %convert_add_fusion.3) | copy-start | bytes 6291460
  264.5 12.7 %collective-permute-start.28 = (bf16[256,1024]{1,0:T(8,128)(2,1)}, bf16[256,1024]{1,0:T(8,128)(2,1)}, u32[]{:S(2)}, u32[]{:S(2)}) collective-permute-start(bf16[256,1024]{1,0:T(8,128)(2,1)} %fusion.108), channel_id=1, source_target_pairs={{0,16},{16,0},{1,17},{17,1},{2,18},{18,2},{3,19},{19,3},{4,20},{20... | collective-permute-start | bytes 1572872 | tf_op jit(solution)/shard_map/ppermute | solution.py:266
  267.4 102.2 %all-to-all-start.7 = ((bf16[4,128,1024]{2,1,0:T(8,128)(2,1)}), bf16[4,128,1024]{2,1,0:T(8,128)(2,1)}, u32[]{:S(2)}, u32[]{:S(2)}) async-start(bf16[4,128,1024]{2,1,0:T(8,128)(2,1)} %bitcast.249), calls=%async_computation.7 | async-start | bytes 2097152 | tf_op jit(solution)/shard_map/all_to_all | solution.py:270
  288.0 14.9 %slice-start = ((s8[11960320]{0:T(1024)(128)(4,1)}), s8[4194304]{0:T(1024)(128)(4,1)S(1)}, s32[]{:S(2)}) async-start(s8[11960320]{0:T(1024)(128)(4,1)} %bitcast.227), calls=%async_computation.9 | async-start | bytes 8388608
  288.0 14.8 %slice-start.1 = ((s8[11960320]{0:T(1024)(128)(4,1)}), s8[4194304]{0:T(1024)(128)(4,1)S(1)}, s32[]{:S(2)}) async-start(s8[11960320]{0:T(1024)(128)(4,1)} %bitcast.227), calls=%async_computation.10 | async-start | bytes 8388608
  294.5 8.4 %slice-start.2 = ((s8[11960320]{0:T(1024)(128)(4,1)}), s8[3571712]{0:T(1024)(128)(4,1)S(1)}, s32[]{:S(2)}) async-start(s8[11960320]{0:T(1024)(128)(4,1)} %bitcast.227), calls=%async_computation.11 | async-start | bytes 7143424
  312.3 8.8 %copy-start.9 = (bf16[8,64,580]{2,1,0:T(8,128)(2,1)S(1)}, bf16[8,64,580]{2,1,0:T(8,128)(2,1)}, u32[]{:S(2)}) copy-start(bf16[8,64,580]{2,1,0:T(8,128)(2,1)} %copy-done.8) | copy-start | bytes 1781764
  314.0 9.5 %copy-start.16 = (bf16[580,1024]{1,0:T(8,128)(2,1)S(1)}, bf16[580,1024]{1,0:T(8,128)(2,1)}, u32[]{:S(2)}) copy-start(bf16[580,1024]{1,0:T(8,128)(2,1)} %copy-done.14) | copy-start | bytes 3563524
  337.2 12.6 %collective-permute-start.29 = (bf16[256,512]{1,0:T(8,128)(2,1)}, bf16[256,512]{1,0:T(8,128)(2,1)}, u32[]{:S(2)}, u32[]{:S(2)}) collective-permute-start(bf16[256,512]{1,0:T(8,128)(2,1)} %convolution_convert_fusion.8), channel_id=1, source_target_pairs={{0,16},{16,0},{1,17},{17,1},{2,18},{18,2},{3,19},{19,3},{4,20},{20... | collective-permute-start | bytes 786440 | tf_op jit(solution)/shard_map/ppermute | solution.py:266
  340.9 12.3 %collective-permute-start.31 = (bf16[256,512]{1,0:T(8,128)(2,1)}, bf16[256,512]{1,0:T(8,128)(2,1)}, u32[]{:S(2)}, u32[]{:S(2)}) collective-permute-start(bf16[256,512]{1,0:T(8,128)(2,1)} %convolution_convert_fusion.7), channel_id=1, source_target_pairs={{0,8},{8,0},{1,9},{9,1},{2,10},{10,2},{3,11},{11,3},{4,12},{12,4},... | collective-permute-start | bytes 786440 | tf_op jit(solution)/shard_map/ppermute | solution.py:262
  343.9 29.5 %collective-permute-start.18 = (bf16[512,768]{1,0:T(8,128)(2,1)}, bf16[512,768]{1,0:T(8,128)(2,1)}, u32[]{:S(2)}, u32[]{:S(2)}) collective-permute-start(bf16[512,768]{1,0:T(8,128)(2,1)} %convolution_convert_fusion.5), channel_id=1, source_target_pairs={{0,16},{16,0},{1,17},{17,1},{2,18},{18,2},{3,19},{19,3},{4,20},{20... | collective-permute-start | bytes 2359304 | tf_op jit(solution)/shard_map/ppermute | solution.py:266
  347.7 29.6 %collective-permute-start.20 = (bf16[512,768]{1,0:T(8,128)(2,1)}, bf16[512,768]{1,0:T(8,128)(2,1)}, u32[]{:S(2)}, u32[]{:S(2)}) collective-permute-start(bf16[512,768]{1,0:T(8,128)(2,1)} %convolution_convert_fusion.4), channel_id=1, source_target_pairs={{0,8},{8,0},{1,9},{9,1},{2,10},{10,2},{3,11},{11,3},{4,12},{12,4},... | collective-permute-start | bytes 2359304 | tf_op jit(solution)/shard_map/ppermute | solution.py:262
  349.8 47.4 %collective-permute-start.16 = (f32[580,640]{1,0:T(8,128)}, f32[580,640]{1,0:T(8,128)}, u32[]{:S(2)}, u32[]{:S(2)}) collective-permute-start(f32[580,640]{1,0:T(8,128)} %select_maximum_fusion), channel_id=1, source_target_pairs={{0,4},{4,0},{1,5},{5,1},{2,6},{6,2},{3,7},{7,3},{8,12},{12,8},{9,1... | collective-permute-start | bytes 4454408 | tf_op jit(solution)/shard_map/ppermute | solution.py:258
  351.6 16.8 %copy-start.25 = (bf16[4,2,32,1024]{3,2,1,0:T(8,128)(2,1)S(1)}, bf16[4,2,32,1024]{3,2,1,0:T(8,128)(2,1)}, u32[]{:S(2)}) copy-start(bf16[4,2,32,1024]{3,2,1,0:T(8,128)(2,1)} %copy.119) | copy-start | bytes 1572868
  351.6 16.8 %copy-start.26 = (bf16[4,2,32,1024]{3,2,1,0:T(8,128)(2,1)S(1)}, bf16[4,2,32,1024]{3,2,1,0:T(8,128)(2,1)}, u32[]{:S(2)}) copy-start(bf16[4,2,32,1024]{3,2,1,0:T(8,128)(2,1)} %copy.120) | copy-start | bytes 1572868
  351.7 16.7 %collective-permute-start.30 = (bf16[128,512]{1,0:T(8,128)(2,1)S(1)}, bf16[128,512]{1,0:T(8,128)(2,1)S(1)}, u32[]{:S(2)}, u32[]{:S(2)}) collective-permute-start(bf16[128,512]{1,0:T(8,128)(2,1)S(1)} %fusion.130), channel_id=1, source_target_pairs={{0,8},{8,0},{1,9},{9,1},{2,10},{10,2},{3,11},{11,3},{4,12},{12,4},... | collective-permute-start | bytes 393224 | tf_op jit(solution)/shard_map/ppermute | solution.py:262
  354.6 13.7 %collective-permute-start.32 = (bf16[128,512]{1,0:T(8,128)(2,1)S(1)}, bf16[128,512]{1,0:T(8,128)(2,1)S(1)}, u32[]{:S(2)}, u32[]{:S(2)}) collective-permute-start(bf16[128,512]{1,0:T(8,128)(2,1)S(1)} %fusion.131), channel_id=1, source_target_pairs={{0,16},{16,0},{1,17},{17,1},{2,18},{18,2},{3,19},{19,3},{4,20},{20... | collective-permute-start | bytes 393224 | tf_op jit(solution)/shard_map/ppermute | solution.py:266
  369.6 18.1 %all-to-all-start.2 = ((bf16[4,145,512]{2,1,0:T(8,128)(2,1)}), bf16[4,145,512]{2,1,0:T(8,128)(2,1)S(1)}, u32[]{:S(2)}, u32[]{:S(2)}) async-start(bf16[4,145,512]{2,1,0:T(8,128)(2,1)} %reshape.1242), calls=%async_computation.2 | async-start | bytes 1245184 | tf_op jit(solution)/shard_map/all_to_all | solution.py:270
  376.3 15.9 %collective-permute-start.19 = (bf16[256,768]{1,0:T(8,128)(2,1)S(1)}, bf16[256,768]{1,0:T(8,128)(2,1)}, u32[]{:S(2)}, u32[]{:S(2)}) collective-permute-start(bf16[256,768]{1,0:T(8,128)(2,1)S(1)} %fusion.112), channel_id=1, source_target_pairs={{0,8},{8,0},{1,9},{9,1},{2,10},{10,2},{3,11},{11,3},{4,12},{12,4},... | collective-permute-start | bytes 1179656 | tf_op jit(solution)/shard_map/ppermute | solution.py:262
  380.2 13.4 %collective-permute-start.21 = (bf16[256,768]{1,0:T(8,128)(2,1)}, bf16[256,768]{1,0:T(8,128)(2,1)}, u32[]{:S(2)}, u32[]{:S(2)}) collective-permute-start(bf16[256,768]{1,0:T(8,128)(2,1)} %fusion.113), channel_id=1, source_target_pairs={{0,16},{16,0},{1,17},{17,1},{2,18},{18,2},{3,19},{19,3},{4,20},{20... | collective-permute-start | bytes 1179656 | tf_op jit(solution)/shard_map/ppermute | solution.py:266
  387.7 34.0 %all-to-all-start.6 = ((bf16[4,160,1024]{2,1,0:T(8,128)(2,1)}), bf16[4,160,1024]{2,1,0:T(8,128)(2,1)}, u32[]{:S(2)}, u32[]{:S(2)}) async-start(bf16[4,160,1024]{2,1,0:T(8,128)(2,1)} %pad_maximum_fusion.4), calls=%async_computation.6 | async-start | bytes 2621440 | tf_op jit(solution)/shard_map/all_to_all | solution.py:270
  392.1 3.5 collective-permute-start.12
  402.7 3.9 collective-permute-start.22
  406.6 4.6 collective-permute-start.23
  421.8 19.6 %all-to-all-start.4 = ((bf16[4,145,512]{2,1,0:T(8,128)(2,1)}), bf16[4,145,512]{2,1,0:T(8,128)(2,1)S(1)}, u32[]{:S(2)}, u32[]{:S(2)}) async-start(bf16[4,145,512]{2,1,0:T(8,128)(2,1)} %reshape.1246), calls=%async_computation.4 | async-start | bytes 1245184 | tf_op jit(solution)/shard_map/all_to_all | solution.py:270
  427.8 17.3 %collective-permute-start.33 = (f32[32,2048]{1,0:T(8,128)}, f32[32,2048]{1,0:T(8,128)}, u32[]{:S(2)}, u32[]{:S(2)}) collective-permute-start(f32[32,2048]{1,0:T(8,128)} %dynamic-slice_bitcast_fusion.4), channel_id=1, source_target_pairs={{0,4},{4,0},{1,5},{5,1},{2,6},{6,2},{3,7},{7,3},{8,12},{12,8},{9,1... | collective-permute-start | bytes 786440 | tf_op jit(solution)/shard_map/ppermute | solution.py:258
  441.4 24.5 %all-to-all-start.5 = ((bf16[4,2,32,1664]{3,2,1,0:T(8,128)(2,1)}), bf16[4,2,32,1664]{3,2,1,0:T(8,128)(2,1)S(1)}, u32[]{:S(2)}, u32[]{:S(2)}) async-start(bf16[4,2,32,1664]{3,2,1,0:T(8,128)(2,1)} %copy.118), calls=%async_computation.5 | async-start | bytes 1703936 | tf_op jit(solution)/shard_map/all_to_all | solution.py:270
  444.9 21.2 %collective-permute-start.17 = (bf16[2,145,512]{2,1,0:T(8,128)(2,1)S(1)}, bf16[2,145,512]{2,1,0:T(8,128)(2,1)S(1)}, u32[]{:S(2)}, u32[]{:S(2)}) collective-permute-start(bf16[2,145,512]{2,1,0:T(8,128)(2,1)S(1)} %get-tuple-element.164), channel_id=1, source_target_pairs={{0,4},{4,0},{1,5},{5,1},{2,6},{6,2},{3,7},{7,3},{8,12},{12,8},{9,1... | collective-permute-start | bytes 890888 | tf_op jit(solution)/shard_map/ppermute | solution.py:258
  466.0 1.7 collective-permute-start.24
  (49 other events, 189.0 us)
Sparse Core Ops, SparseCore 0:
  16.5 157.7 all-gather.2
